TPU v7x, 512 devices: a whole 4x8x8 slice. The times are simulated.
512 devices in a mesh: member: 16 (over x, y_lo), lat: 32 (over z, y_hi, core).
Axes of the slice: x: 4, y: 8 (y_hi: 2, y_lo: 4; y = y_hi * 4 + y_lo), z: 8, core: 2. Of those that a mesh axis runs over, the one named last changes fastest.
Arguments:
- states: bfloat16 [16, 64, 256, 256], P('member', 'lat'), may hold values from -6 to 6
- member_id: int32 [16], P('member'), may hold values from 0 to 15, each once
- member_gain: float32 [16, 256], replicated, may hold values from 0.5 to 2
- first_conv: bfloat16 [2304, 256], P('member'), may hold values from -0.125 to 0.125
- second_conv: bfloat16 [2304, 256], P('member'), may hold values from -0.125 to 0.125
- head: bfloat16 [256, 8], replicated, may hold values from -0.375 to 0.375
- target: float32 [8, 64, 256], P(None, 'lat'), may hold values from -6 to 6
- lat_start: int32 [1], replicated, may hold values from 0 to 1737
Outputs:
- score: float32 [8, 64, 256], P(None, 'lat')
- mean_score: float32 [], replicated
All inputs are finite; a program needn't handle non-finite values.
Results may differ from a plain program's by a relative error of at most 0.0018.
Values may be sent and summed in bfloat16 or wider, within the bound.
No kernel may reach another device: no remote copies, remote signals or barrier semaphores. Data moves between devices by JAX's collectives and lax.ppermute only.
A program may use at most 64 MiB of HBM per device.

v0:
```python
import jax
import jax.numpy as jnp
from jax import lax
from jax.sharding import PartitionSpec as P


def with_halo(block, sides, width):
    for axis, dim in sides:
        count = lax.axis_size(axis)
        forward = [(i, i + 1) for i in range(count - 1)]
        backward = [(target, source) for source, target in forward]
        low = lax.ppermute(
            lax.slice_in_dim(block, block.shape[dim] - width, None, axis=dim), axis, forward
        )
        high = lax.ppermute(lax.slice_in_dim(block, 0, width, axis=dim), axis, backward)
        block = jnp.concatenate([low, block, high], axis=dim)
    return block


def product(left, right):
    return jnp.dot(
        left.astype(jnp.float32),
        right.astype(jnp.float32),
        precision=lax.Precision.HIGHEST,
        preferred_element_type=jnp.float32,
    )


def patch_rows(field):
    rows, cols, chans = (field.shape[0] - 2, field.shape[1], field.shape[2])
    padded = jnp.pad(field, ((0, 0), (1, 1), (0, 0)))
    taps = [padded[dy : dy + rows, dx : dx + cols, :] for dy in range(3) for dx in range(3)]
    return jnp.concatenate(taps, axis=-1).reshape(rows * cols, 9 * chans)


def folded_conv(patches, weight_rows):
    return product(patches, lax.all_gather(weight_rows, "member", axis=0, tiled=True))


def body(states, member_id, member_gain, first_conv, second_conv, head, target, lat_start):
    rows, cols, chans = (states.shape[1], states.shape[2], states.shape[3])
    members = lax.axis_size("member")
    band = lax.axis_index("lat")
    select = (jnp.arange(members, dtype=jnp.int32)[None, :] == member_id[:, None]).astype(
        jnp.float32
    )
    gain = jnp.dot(select, member_gain, precision=lax.Precision.HIGHEST)
    start = (states[0].astype(jnp.float32) * gain[0]).astype(jnp.bfloat16)

    def with_rims(field):
        return with_halo(field, (("lat", 0),), 1)

    first_out = folded_conv(patch_rows(with_rims(start)), first_conv)
    inner = jax.nn.gelu(first_out, approximate=True).astype(jnp.bfloat16).reshape(rows, cols, -1)
    second_out = folded_conv(patch_rows(with_rims(inner)), second_conv)
    block = (start.reshape(rows * cols, chans).astype(jnp.float32) + second_out).astype(
        jnp.bfloat16
    )
    pred = product(block, head)
    pred = pred.T.reshape(-1, rows, cols).astype(jnp.bfloat16)
    eps = 0.05 / members
    factor = (1.0 - eps) / (2.0 * members * (members - 1))
    fields = lax.all_gather(pred[None], "member", axis=0, tiled=True).astype(jnp.float32)
    skill = jnp.sum(jnp.abs(fields - target[None]), axis=0) / members

    def pair_step(index, total):
        chosen = lax.dynamic_index_in_dim(fields, index, 0, keepdims=True)
        return total + jnp.sum(jnp.abs(chosen - fields), axis=0)

    spread = lax.fori_loop(0, members, pair_step, jnp.zeros_like(skill))
    score = skill - factor * spread
    row_ids = lat_start[0] + band * rows + jnp.arange(rows, dtype=jnp.int32)
    area = jnp.cos(jnp.pi * (90.0 - 0.1 * row_ids.astype(jnp.float32)) / 180.0)
    weighted, area_total = lax.psum((jnp.sum(score * area[None, :, None]), jnp.sum(area)), "lat")
    mean_score = weighted / (score.shape[0] * cols * area_total)
    return (score, mean_score)


def solution(mesh):
    placed = (
        P("member", "lat", None, None),
        P("member"),
        P(),
        P("member", None),
        P("member", None),
        P(),
        P(None, "lat", None),
        P(),
    )
    return jax.shard_map(
        body, mesh=mesh, in_specs=placed, out_specs=(P(None, "lat", None), P()), check_vma=False
    )
```

profile of v0, /device:TPU:1, one launch (start us, length us, event | category | flops | bytes accessed | tf_op | source)
XLA Modules:
  0.0 331.9 jit_solution(7354187665463545966)
XLA Ops:
  8.7 1.0 fusion.15
  9.8 8.8 %collective-permute-start = (bf16[1,256,256]{2,1,0:T(8,128)(2,1)S(1)}, bf16[1,256,256]{2,1,0:T(8,128)(2,1)S(1)}, u32[]{:S(2)}, u32[]{:S(2)}) collective-permute-start(bf16[1,256,256]{2,1,0:T(8,128)(2,1)S(1)} %get-tuple-element.107), channel_id=1, source_target_pairs={{0,1},{1,2},{2,3},{3,4},{4,5},{5,6},{6,7},{7,8},{8,9},{9,10},{10,1... | collective-permute-start | bytes 393224 | tf_op jit(solution)/shard_map/ppermute | solution.py:12
  18.6 1.9 collective-permute-start.1
  20.6 8.2 %collective-permute-done.1 = bf16[1,256,256]{2,1,0:T(8,128)(2,1)S(1)} collective-permute-done((bf16[1,256,256]{2,1,0:T(8,128)(2,1)S(1)}, bf16[1,256,256]{2,1,0:T(8,128)(2,1)S(1)}, u32[]{:S(2)}, u32[]{:S(2)}) %collective-permute-start.1) | collective-permute-done | bytes 131104 | tf_op jit(solution)/shard_map/ppermute | solution.py:15
  29.4 61.0 %all-gather.3.cloned.1.call-done = bf16[2304,256]{1,0:T(8,128)(2,1)} async-done(((bf16[144,256]{1,0:T(8,128)(2,1)}), bf16[2304,256]{1,0:T(8,128)(2,1)}) %all-gather.3.cloned.1.call-update) | async-done | bytes 1179664 | tf_op jit(solution)/shard_map/all_gather | solution.py:37
  90.4 2.1 fusion.14
  92.5 17.7 %collective-permute-start.2 = (bf16[1,256,256]{2,1,0:T(8,128)(2,1)S(1)}, bf16[1,256,256]{2,1,0:T(8,128)(2,1)S(1)}, u32[]{:S(2)}, u32[]{:S(2)}) collective-permute-start(bf16[1,256,256]{2,1,0:T(8,128)(2,1)S(1)} %get-tuple-element.105), channel_id=1, source_target_pairs={{0,1},{1,2},{2,3},{3,4},{4,5},{5,6},{6,7},{7,8},{8,9},{9,10},{10,1... | collective-permute-start | bytes 393224 | tf_op jit(solution)/shard_map/ppermute | solution.py:12
  110.2 1.9 collective-permute-start.3
  112.9 0.7 fusion.25
  113.7 6.8 %collective-permute-done.3 = bf16[1,256,256]{2,1,0:T(8,128)(2,1)S(1)} collective-permute-done((bf16[1,256,256]{2,1,0:T(8,128)(2,1)S(1)}, bf16[1,256,256]{2,1,0:T(8,128)(2,1)S(1)}, u32[]{:S(2)}, u32[]{:S(2)}) %collective-permute-start.3) | collective-permute-done | bytes 131104 | tf_op jit(solution)/shard_map/ppermute | solution.py:15
  120.8 0.8 constant_dynamic-update-slice_fusion.9
  121.7 0.8 constant_dynamic-update-slice_fusion.8
  122.4 0.7 constant_dynamic-update-slice_fusion.7
  123.2 0.7 constant_dynamic-update-slice_fusion.6
  123.9 0.8 constant_dynamic-update-slice_fusion.5
  124.7 0.7 constant_dynamic-update-slice_fusion.4
  125.4 0.7 constant_dynamic-update-slice_fusion.3
  126.1 0.8 constant_dynamic-update-slice_fusion.2
  126.9 0.8 constant_dynamic-update-slice_fusion.1
  127.7 48.5 %all-gather.5.cloned.1.call-done = bf16[2304,256]{1,0:T(8,128)(2,1)} async-done(((bf16[144,256]{1,0:T(8,128)(2,1)}), bf16[2304,256]{1,0:T(8,128)(2,1)}) %all-gather.5.cloned.1.call-update) | async-done | bytes 1179664 | tf_op jit(solution)/shard_map/all_gather | solution.py:37
  176.2 2.8 fusion
  179.2 36.0 %all_gather.11 = bf16[16,8,2,256]{3,1,2,0:T(8,128)(2,1)S(1)} all-gather(bf16[1,8,2,256]{3,1,2,0:T(8,128)(2,1)S(1)} %bitcast.56), channel_id=1, replica_groups=mesh['member'=16,'lat'=32] {'member'}, dimensions={0}, use_global_device_ids=true | all-gather | bytes 139264 | tf_op jit(solution)/shard_map/all_gather | solution.py:63
  215.3 3.4 %while.14 = (s32[]{:T(128)}, f32[8,2,256]{2,1,0:T(2,128)S(1)}, f32[16,8,2,256]{3,2,1,0:T(2,128)S(1)}, s32[]{:T(128)}, s32[]{:T(128)}) while((s32[]{:T(128)}, f32[8,2,256]{2,1,0:T(2,128)S(1)}, f32[16,8,2,256]{3,2,1,0:T(2,128)S(1)}, s32[]{:T(128)}, s32[]{:T(128)}) %tuple.48), condition=%wide.region_3.4_spmd.clone, body=%wide.region_1.3_spmd.clone.sunk | while | flops 200707 | bytes 376907 | solution.py:70
  220.1 102.5 %all-reduce.2 = (f32[]{:T(128)}, f32[]{:T(128)}) all-reduce(f32[]{:T(128)} %get-tuple-element.95, f32[]{:T(128)} %fusion.25), channel_id=1, replica_groups=mesh['member'=16,'lat'=32] {'lat'}, use_global_device_ids=true, to_apply=%region_5.6 | all-reduce | flops 2 | bytes 16 | tf_op jit(solution)/shard_map/psum | solution.py:74
  (87 shorter events, 6.5 us)
Async XLA Ops:
  7.2 1.5 copy-start
  7.2 21.9 %copy-start.1 = (bf16[1,2,256,256]{3,2,1,0:T(8,128)(2,1)S(1)}, bf16[1,2,256,256]{3,2,1,0:T(8,128)(2,1)}, u32[]{:S(2)}) copy-start(bf16[1,2,256,256]{3,2,1,0:T(8,128)(2,1)} %param.10) | copy-start | bytes 786436
  7.2 83.2 %all-gather.3.cloned.1.call-start = ((), (), s32[]{:S(2)}) async-start(), calls=%async_computation | async-start | bytes 1253376 | tf_op jit(solution)/shard_map/all_gather | solution.py:37
  7.9 168.3 %all-gather.5.cloned.1.call-start = ((), (), s32[]{:S(2)}) async-start(), calls=%async_computation.1 | async-start | bytes 1253376 | tf_op jit(solution)/shard_map/all_gather | solution.py:37
  9.8 10.8 %collective-permute-start = (bf16[1,256,256]{2,1,0:T(8,128)(2,1)S(1)}, bf16[1,256,256]{2,1,0:T(8,128)(2,1)S(1)}, u32[]{:S(2)}, u32[]{:S(2)}) collective-permute-start(bf16[1,256,256]{2,1,0:T(8,128)(2,1)S(1)} %get-tuple-element.107), channel_id=1, source_target_pairs={{0,1},{1,2},{2,3},{3,4},{4,5},{5,6},{6,7},{7,8},{8,9},{9,10},{10,1... | collective-permute-start | bytes 393224 | tf_op jit(solution)/shard_map/ppermute | solution.py:12
  18.6 10.2 %collective-permute-start.1 = (bf16[1,256,256]{2,1,0:T(8,128)(2,1)S(1)}, bf16[1,256,256]{2,1,0:T(8,128)(2,1)S(1)}, u32[]{:S(2)}, u32[]{:S(2)}) collective-permute-start(bf16[1,256,256]{2,1,0:T(8,128)(2,1)S(1)} %get-tuple-element.108), channel_id=1, source_target_pairs={{1,0},{2,1},{3,2},{4,3},{5,4},{6,5},{7,6},{8,7},{9,8},{10,9},{11,1... | collective-permute-start | bytes 393224 | tf_op jit(solution)/shard_map/ppermute | solution.py:15
  90.4 21.8 %copy-start.2 = (f32[8,2,256]{2,1,0:T(2,128)S(1)}, f32[8,2,256]{2,1,0:T(2,128)}, u32[]{:S(2)}) copy-start(f32[8,2,256]{2,1,0:T(2,128)} %param.16) | copy-start | bytes 49156
  92.5 21.1 %collective-permute-start.2 = (bf16[1,256,256]{2,1,0:T(8,128)(2,1)S(1)}, bf16[1,256,256]{2,1,0:T(8,128)(2,1)S(1)}, u32[]{:S(2)}, u32[]{:S(2)}) collective-permute-start(bf16[1,256,256]{2,1,0:T(8,128)(2,1)S(1)} %get-tuple-element.105), channel_id=1, source_target_pairs={{0,1},{1,2},{2,3},{3,4},{4,5},{5,6},{6,7},{7,8},{8,9},{9,10},{10,1... | collective-permute-start | bytes 393224 | tf_op jit(solution)/shard_map/ppermute | solution.py:12
  110.2 10.3 %collective-permute-start.3 = (bf16[1,256,256]{2,1,0:T(8,128)(2,1)S(1)}, bf16[1,256,256]{2,1,0:T(8,128)(2,1)S(1)}, u32[]{:S(2)}, u32[]{:S(2)}) collective-permute-start(bf16[1,256,256]{2,1,0:T(8,128)(2,1)S(1)} %get-tuple-element.106), channel_id=1, source_target_pairs={{1,0},{2,1},{3,2},{4,3},{5,4},{6,5},{7,6},{8,7},{9,8},{10,9},{11,1... | collective-permute-start | bytes 393224 | tf_op jit(solution)/shard_map/ppermute | solution.py:15
  127.7 51.3 %copy-start.3 = (bf16[256,8]{0,1:T(8,128)(2,1)S(1)}, bf16[256,8]{0,1:T(8,128)(2,1)}, u32[]{:S(2)}) copy-start(bf16[256,8]{0,1:T(8,128)(2,1)} %param.15) | copy-start | bytes 12292
Sparse Core Ops, SparseCore 0:
  10.1 80.2 all-gather.2
  92.5 83.7 all-gather.4
where the time goes:
time: 332 us
  blocking collectives  139 us (42%)
  waiting for transfers between devices  125 us (38%)
  starting transfers between devices  30.4 us (9%)
  between operations  18.1 us (5%)
  local copies, waits for them, and re-layouts  8.13 us (2%)
  other arithmetic  5.8 us (2%)
  matrix products  5.15 us (2%)
    all_gather x2, waiting for transfers between devices, folded_conv(): lax.all_gather(weight_rows, 'member', axis=0, tiled=True)  110 us
    psum x1, blocking collectives, body(): lax.psum((jnp.sum(score * area[None, :, None]), jnp.sum(area)), 'lat')  102 us
    all_gather x1, blocking collectives, body(): lax.all_gather(pred[None], 'member', axis=0, tiled=True).astype(jnp.float32)  36 us
    ppermute x2, starting transfers between devices, with_halo(): lax.ppermute(lax.slice_in_dim(block, block.shape[dim] - width, None, axis...  26.5 us
    ppermute x2, waiting for transfers between devices, with_halo(): lax.ppermute(lax.slice_in_dim(block, 0, width, axis=dim), axis, backward)  15.1 us
    unnamed x24, local copies, waits for them, and re-layouts  6.93 us
  transfers between devices with their start and end apart: 6, of which 4 were waited for; matrix products, arithmetic and copies ran while one was open for 4% of the time, Pallas kernels for 0%

commit v1 on v0

v1 whole, which is shorter than its diff:
```python
import functools

import jax
import jax.numpy as jnp
from jax import lax
from jax.experimental import pallas as pl
from jax.experimental.pallas import tpu as pltpu
from jax.sharding import PartitionSpec as P

MEMBERS, BANDS = 16, 32
AXES = ("member", "lat")


def partner_in_y(member, lat, flip):
    low, high = member % 4, lat // 2 % 2
    if flip == 1:
        return member ^ 1, lat
    return member ^ 3, lat ^ 2 if low in (0, 3) else lat


def partner_in_x(member, lat, flip):
    return member ^ (4 * flip), lat


def pairing(partner, step):
    pairs = []
    for member in range(MEMBERS):
        for lat in range(BANDS):
            flip = (1, 3)[(lat + step) % 2]
            other = partner(member, lat, flip)
            pairs.append((member * BANDS + lat, other[0] * BANDS + other[1]))
    return pairs


def swap(block, partner, step):
    return lax.ppermute(block, AXES, pairing(partner, step))


def tap_sum(shifted, weights, first, rows):
    cols, chans = shifted.shape[2], shifted.shape[3]
    total = None
    for dy in range(3):
        for dx in range(3):
            left = shifted[dx, first + dy : first + dy + rows].reshape(rows * cols, chans)
            base = (dy * 3 + dx) * chans
            right = jnp.concatenate(
                [weights[0, base : base + chans], weights[1, base : base + chans]], axis=1
            )
            term = jnp.dot(left, right, preferred_element_type=jnp.float32)
            total = term if total is None else total + term
    return total


def put_shifted(shifted, row, value):
    cols = value.shape[0]
    column = lax.broadcasted_iota(jnp.int32, value.shape, 0)
    before = jnp.where(column == 0, 0.0, pltpu.roll(value, 1, 0))
    after = jnp.where(column == cols - 1, 0.0, pltpu.roll(value, cols - 1, 0))
    shifted[0, row] = before.astype(jnp.bfloat16)
    shifted[1, row] = value.astype(jnp.bfloat16)
    shifted[2, row] = after.astype(jnp.bfloat16)


def put_weights(weights, core, member, blocks, depth):
    turns = jnp.where(core == 0, 1, 3)
    masks = (0, turns, turns ^ 2, 2)
    at = 0
    for ref in blocks:
        for index in range(ref.shape[0]):
            mask = masks[at // 4] * 4 + masks[at % 4]
            origin = (member ^ mask) * depth
            weights[core, pl.ds(pl.multiple_of(origin, 16), depth), :] = ref[index]
            at += 1


def first_kernel(
    ident, gains, own, near, far, mine_a, mine_b, other_a, other_b, inner, shifted, weights
):
    member, lat = lax.axis_index("member"), lax.axis_index("lat")
    core = lat % 2
    depth = mine_a.shape[1]
    gain = gains[pl.ds(ident[0], 1), :]
    rows = own.shape[0]
    for ref, base in ((own, rows), (near, 2 * rows * (1 - core)), (far, 2 * rows * core)):
        for row in range(rows):
            value = (ref[row].astype(jnp.float32) * gain).astype(jnp.bfloat16)
            put_shifted(shifted, base + row, value.astype(jnp.float32))
    put_weights(weights, core, member, (mine_a, mine_b), depth)
    put_weights(weights, 1 - core, member, (other_a, other_b), depth)
    for half in range(2):
        out = tap_sum(shifted, weights, 2 * half, 2)
        out = jax.nn.gelu(out, approximate=True)
        out = out.reshape(2, out.shape[0] // 2, out.shape[1])
        for row in range(2):
            value = out[row]
            if half == 0 and row == 0:
                value = jnp.where(lat == 0, 0.0, value)
            if half == 1 and row == 1:
                value = jnp.where(lat == BANDS - 1, 0.0, value)
            inner[2 * half + row] = value.astype(jnp.bfloat16)


def second_kernel(
    ident, gains, own, inner, head, mine_a, mine_b, other_a, other_b, pred, shifted, weights
):
    member, lat = lax.axis_index("member"), lax.axis_index("lat")
    core = lat % 2
    depth = mine_a.shape[1]
    gain = gains[pl.ds(ident[0], 1), :]
    for row in range(inner.shape[0]):
        put_shifted(shifted, row, inner[row].astype(jnp.float32))
    put_weights(weights, core, member, (mine_a, mine_b), depth)
    put_weights(weights, 1 - core, member, (other_a, other_b), depth)
    rows, cols, chans = own.shape
    out = tap_sum(shifted, weights, 0, rows)
    start = (own[...].reshape(rows * cols, chans).astype(jnp.float32) * gain).astype(jnp.bfloat16)
    block = (start.astype(jnp.float32) + out).astype(jnp.bfloat16)
    value = lax.dot_general(
        head[...], block, (((1,), (1,)), ((), ())), preferred_element_type=jnp.float32
    ).astype(jnp.bfloat16)
    for index in range(pred.shape[0]):
        pred[index] = value


def score_kernel(weight, fields, target, score, partial, *, factor):
    members = fields.shape[0]
    cols = target.shape[2]
    parts = []
    for row in range(target.shape[1]):
        span = slice(row * cols, (row + 1) * cols)
        values = [fields[m, :, span].astype(jnp.float32) for m in range(members)]
        truth = target[:, row, :]
        skill = functools.reduce(jnp.add, [jnp.abs(v - truth) for v in values])
        spread = functools.reduce(
            jnp.add,
            [
                functools.reduce(jnp.add, [jnp.abs(values[m] - values[n]) for n in range(m)])
                for m in range(1, members)
            ],
        )
        result = skill / members - (2.0 * factor) * spread
        score[:, row, :] = result
        parts.append(jnp.sum(result) * weight[row])
    partial[...] = jnp.full(partial.shape, functools.reduce(jnp.add, parts), jnp.float32)


VMEM = pl.BlockSpec(memory_space=pltpu.VMEM)
SMEM = pl.BlockSpec(memory_space=pltpu.SMEM)


def body(states, member_id, member_gain, first_conv, second_conv, head, target, lat_start):
    rows, cols, chans = (states.shape[1], states.shape[2], states.shape[3])
    depth = first_conv.shape[0]
    lat = lax.axis_index("lat")
    core = lat % 2
    own = states[0]

    half = chans // 2
    shard = jnp.stack([first_conv, second_conv])
    mine = jnp.where(core == 0, shard[:, :, :half], shard[:, :, half:])[None]
    mine = jnp.concatenate([mine, swap(mine, partner_in_y, 0)], axis=0)
    mine = jnp.concatenate([mine, swap(mine, partner_in_y, 1)], axis=0)
    mine = jnp.concatenate([mine, swap(mine, partner_in_x, 0)], axis=0)
    first_a, second_a = mine[:, 0], mine[:, 1]
    first_b = swap(first_a, partner_in_x, 1)
    second_b = swap(second_a, partner_in_x, 1)

    on_chip = [(lat_id, lat_id ^ 1) for lat_id in range(BANDS)]
    across = [(lat_id, ((lat_id + 1) ^ 1) - 1) for lat_id in range(1, BANDS - 1)]
    near = lax.ppermute(own, "lat", on_chip)
    far = lax.ppermute(own, "lat", across)
    others = [lax.ppermute(block, "lat", on_chip) for block in (first_a, first_b, second_a, second_b)]

    inner = pl.pallas_call(
        first_kernel,
        out_shape=jax.ShapeDtypeStruct((rows + 2, cols, chans), jnp.bfloat16),
        in_specs=[SMEM] + [VMEM] * 8,
        out_specs=VMEM,
        scratch_shapes=[
            pltpu.VMEM((3, 3 * rows, cols, chans), jnp.bfloat16),
            pltpu.VMEM((2, 9 * chans, half), jnp.bfloat16),
        ],
        cost_estimate=pl.CostEstimate(
            flops=2 * (rows + 2) * cols * 9 * chans * chans, bytes_accessed=4 << 20, transcendentals=0
        ),
        name="first",
    )(member_id, member_gain, own, near, far, first_a, first_b, others[0], others[1])
    pred = pl.pallas_call(
        second_kernel,
        out_shape=jax.ShapeDtypeStruct((MEMBERS, head.shape[1], rows * cols), jnp.bfloat16),
        in_specs=[SMEM] + [VMEM] * 8,
        out_specs=VMEM,
        scratch_shapes=[
            pltpu.VMEM((3, rows + 2, cols, chans), jnp.bfloat16),
            pltpu.VMEM((2, 9 * chans, half), jnp.bfloat16),
        ],
        cost_estimate=pl.CostEstimate(
            flops=2 * rows * cols * 9 * chans * chans, bytes_accessed=3 << 20, transcendentals=0
        ),
        name="second",
    )(member_id, member_gain, own, inner, head.T, second_a, second_b, others[2], others[3])
    fields = lax.all_to_all(pred, "member", 0, 0, tiled=True)

    row_ids = lat_start[0] + jnp.arange(BANDS * rows, dtype=jnp.int32)
    area = jnp.cos(jnp.pi * (90.0 - 0.1 * row_ids.astype(jnp.float32)) / 180.0)
    weight = lax.dynamic_slice(area, (lat * rows,), (rows,)) / (
        head.shape[1] * cols * jnp.sum(area)
    )
    eps = 0.05 / MEMBERS
    factor = (1.0 - eps) / (2.0 * MEMBERS * (MEMBERS - 1))
    score, partial = pl.pallas_call(
        functools.partial(score_kernel, factor=factor),
        out_shape=(
            jax.ShapeDtypeStruct(target.shape, jnp.float32),
            jax.ShapeDtypeStruct((BANDS, 1, 128), jnp.float32),
        ),
        in_specs=[SMEM, VMEM, VMEM],
        out_specs=(VMEM, VMEM),
        name="score",
    )(weight, fields, target)
    shares = lax.all_to_all(partial, "lat", 0, 0, tiled=True)
    return (score, jnp.sum(shares[:, 0, 0]))


def solution(mesh):
    assert mesh.shape["member"] == MEMBERS and mesh.shape["lat"] == BANDS
    placed = (
        P("member", "lat", None, None),
        P("member"),
        P(),
        P("member", None),
        P("member", None),
        P(),
        P(None, "lat", None),
        P(),
    )
    return jax.shard_map(
        body, mesh=mesh, in_specs=placed, out_specs=(P(None, "lat", None), P()), check_vma=False
    )
```

time: 332 us -> 114 us (0.34)
  blocking collectives: 139 us -> 28.5 us
  waiting for transfers between devices: 125 us -> 20.2 us
  starting transfers between devices: 30.4 us -> 46.5 us
  between operations: 18.1 us -> 2.85 us
  Pallas kernels: 0 us -> 9.35 us
  matrix products: 5.15 us -> 0 us
  local copies, waits for them, and re-layouts: 8.13 us -> 3.04 us
    all_gather x2 -> x0, waiting for transfers between devices: 110 us -> none  [folded_conv(): lax.all_gather(weight_rows, 'member', axis=0, tiled=True)]
    psum x1 -> x0, blocking collectives: 102 us -> none  [body(): lax.psum((jnp.sum(score * area[None, :, None]), jnp.sum(area)), 'lat')]
    all_gather x1 -> x0, blocking collectives: 36 us -> none  [body(): lax.all_gather(pred[None], 'member', axis=0, tiled=True).astype(jnp.float32)]
    all_to_all x0 -> x1, blocking collectives: none -> 28.5 us  [body(): shares = lax.all_to_all(partial, 'lat', 0, 0, tiled=True)]
    ppermute x4 -> x11, starting transfers between devices: 30.4 us -> 41.7 us  [the longest x5 17.1 us: swap(): return lax.ppermute(block, AXES, pairing(partner, step))]
    pallas_call x0 -> x3, Pallas kernels: none -> 9.35 us  [the longest x1 4.26 us: body(): pl.pallas_call(first_kernel, out_shape=jax.ShapeDtypeStruct((rows + 2, co...]
    dot_general x4 -> x0, matrix products: 5.15 us -> none  [the longest x3 5.04 us: product(): jnp.dot(left.astype(jnp.float32), right.astype(jnp.float32), precision=la...]
    all_to_all x0 -> x1, starting transfers between devices: none -> 4.8 us  [body(): fields = lax.all_to_all(pred, 'member', 0, 0, tiled=True)]
  transfers between devices with their start and end apart: 6 -> 12, of which waited for: 4 -> 5; matrix products, arithmetic and copies ran while one was open for 4% -> 1% of each run, Pallas kernels for 0% -> 4%
where the time goes in v1:
time: 114 us; the launch traced here: 113 us
  starting transfers between devices  46.5 us (41%)
  blocking collectives  28.5 us (25%)
  waiting for transfers between devices  20.2 us (18%)
  Pallas kernels  9.35 us (8%)
  local copies, waits for them, and re-layouts  3.04 us (3%)
  other arithmetic  2.87 us (3%)
  between operations  2.85 us (2%)
    all_to_all x1, blocking collectives, body(): shares = lax.all_to_all(partial, 'lat', 0, 0, tiled=True)  28.5 us
    ppermute x5, starting transfers between devices, swap(): return lax.ppermute(block, AXES, pairing(partner, step))  17.1 us
    ppermute x1, starting transfers between devices, body(): near = lax.ppermute(own, 'lat', on_chip)  14 us
    ppermute x5, waiting for transfers between devices, swap(): return lax.ppermute(block, AXES, pairing(partner, step))  10.8 us
    ppermute x4, starting transfers between devices, body(): lax.ppermute(block, 'lat', on_chip)  8.65 us
    all_to_all x1, starting transfers between devices, body(): fields = lax.all_to_all(pred, 'member', 0, 0, tiled=True)  4.8 us
    ppermute x1, waiting for transfers between devices, body(): far = lax.ppermute(own, 'lat', across)  4.74 us
    all_to_all x1, waiting for transfers between devices, body(): fields = lax.all_to_all(pred, 'member', 0, 0, tiled=True)  4.67 us
  transfers between devices with their start and end apart: 12, of which 5 were waited for; matrix products, arithmetic and copies ran while one was open for 1% of the time, Pallas kernels for 4%

profile of v1, /device:TPU:1, one launch (start us, length us, event | category | flops | bytes accessed | tf_op | source)
XLA Modules:
  0.0 113.3 jit_solution(16969689590906961715)
XLA Ops:
  0.6 0.8 fusion.2
  1.5 5.9 %collective-permute-start.2 = (bf16[1,2,144,128]{3,2,0,1:T(8,128)(2,1)S(1)}, bf16[1,2,144,128]{3,2,0,1:T(8,128)(2,1)S(1)}, u32[]{:S(2)}, u32[]{:S(2)}) collective-permute-start(bf16[1,2,144,128]{3,2,0,1:T(8,128)(2,1)S(1)} %fusion.2), channel_id=1, source_target_pairs={{0,32},{1,99},{2,34},{3,97},{4,36},{5,103},{6,38},{7,101},{8,40},{... | collective-permute-start | bytes 221192 | tf_op jit(solution)/shard_map/ppermute | solution.py:36
  7.4 1.7 %collective-permute-done.2 = bf16[1,2,144,128]{3,2,0,1:T(8,128)(2,1)S(1)} collective-permute-done((bf16[1,2,144,128]{3,2,0,1:T(8,128)(2,1)S(1)}, bf16[1,2,144,128]{3,2,0,1:T(8,128)(2,1)S(1)}, u32[]{:S(2)}, u32[]{:S(2)}) %collective-permute-start.2) | collective-permute-done | bytes 73760 | tf_op jit(solution)/shard_map/ppermute | solution.py:36
  9.2 1.9 %collective-permute-start.3 = (bf16[2,2,144,128]{3,2,0,1:T(8,128)(2,1)S(1)}, bf16[2,2,144,128]{3,2,0,1:T(8,128)(2,1)S(1)}, u32[]{:S(2)}, u32[]{:S(2)}) collective-permute-start(bf16[2,2,144,128]{3,2,0,1:T(8,128)(2,1)S(1)} %pad_maximum_fusion.2), channel_id=1, source_target_pairs={{0,98},{1,33},{2,96},{3,35},{4,102},{5,37},{6,100},{7,39},{8,106},... | collective-permute-start | bytes 442376 | tf_op jit(solution)/shard_map/ppermute | solution.py:36
  11.1 4.4 %collective-permute-done.3 = bf16[2,2,144,128]{3,2,0,1:T(8,128)(2,1)S(1)} collective-permute-done((bf16[2,2,144,128]{3,2,0,1:T(8,128)(2,1)S(1)}, bf16[2,2,144,128]{3,2,0,1:T(8,128)(2,1)S(1)}, u32[]{:S(2)}, u32[]{:S(2)}) %collective-permute-start.3) | collective-permute-done | bytes 147488 | tf_op jit(solution)/shard_map/ppermute | solution.py:36
  15.5 4.0 %collective-permute-start.4 = (bf16[4,2,144,128]{3,2,0,1:T(8,128)(2,1)S(1)}, bf16[4,2,144,128]{3,2,0,1:T(8,128)(2,1)S(1)}, u32[]{:S(2)}, u32[]{:S(2)}) collective-permute-start(bf16[4,2,144,128]{3,2,0,1:T(8,128)(2,1)S(1)} %pad_maximum_fusion.1), channel_id=1, source_target_pairs={{0,128},{1,385},{2,130},{3,387},{4,132},{5,389},{6,134},{7,391},{8... | collective-permute-start | bytes 884744 | tf_op jit(solution)/shard_map/ppermute | solution.py:36
  19.5 4.7 %collective-permute-done.4 = bf16[4,2,144,128]{3,2,0,1:T(8,128)(2,1)S(1)} collective-permute-done((bf16[4,2,144,128]{3,2,0,1:T(8,128)(2,1)S(1)}, bf16[4,2,144,128]{3,2,0,1:T(8,128)(2,1)S(1)}, u32[]{:S(2)}, u32[]{:S(2)}) %collective-permute-start.4) | collective-permute-done | bytes 294944 | tf_op jit(solution)/shard_map/ppermute | solution.py:36
  24.3 1.9 %collective-permute-start.5 = (bf16[8,144,128]{2,1,0:T(8,128)(2,1)S(1)}, bf16[8,144,128]{2,1,0:T(8,128)(2,1)S(1)}, u32[]{:S(2)}, u32[]{:S(2)}) collective-permute-start(bf16[8,144,128]{2,1,0:T(8,128)(2,1)S(1)} %get-tuple-element.7.mine_a), channel_id=1, source_target_pairs={{0,384},{1,129},{2,386},{3,131},{4,388},{5,133},{6,390},{7,135},{8... | collective-permute-start | bytes 884744 | tf_op jit(solution)/shard_map/ppermute | solution.py:36
  26.3 3.4 %collective-permute-start.8 = (bf16[8,144,128]{2,1,0:T(8,128)(2,1)S(1)}, bf16[8,144,128]{2,1,0:T(8,128)(2,1)S(1)}, u32[]{:S(2)}, u32[]{:S(2)}) collective-permute-start(bf16[8,144,128]{2,1,0:T(8,128)(2,1)S(1)} %get-tuple-element.6.mine_a), channel_id=1, source_target_pairs={{0,384},{1,129},{2,386},{3,131},{4,388},{5,133},{6,390},{7,135},{8... | collective-permute-start | bytes 884744 | tf_op jit(solution)/shard_map/ppermute | solution.py:36
  29.6 14.0 %collective-permute-start = (bf16[2,256,256]{2,1,0:T(8,128)(2,1)S(1)}, bf16[2,256,256]{2,1,0:T(8,128)(2,1)S(1)}, u32[]{:S(2)}, u32[]{:S(2)}) collective-permute-start(bf16[2,256,256]{2,1,0:T(8,128)(2,1)S(1)} %bitcast.17), channel_id=1, source_target_pairs={{0,1},{1,0},{2,3},{3,2},{4,5},{5,4},{6,7},{7,6},{8,9},{9,8},{10,11... | collective-permute-start | bytes 786440 | tf_op jit(solution)/shard_map/ppermute | solution.py:170
  43.6 1.9 %collective-permute-start.6 = (bf16[8,144,128]{2,1,0:T(8,128)(2,1)S(1)}, bf16[8,144,128]{2,1,0:T(8,128)(2,1)S(1)}, u32[]{:S(2)}, u32[]{:S(2)}) collective-permute-start(bf16[8,144,128]{2,1,0:T(8,128)(2,1)S(1)} %get-tuple-element.7.mine_a), channel_id=1, source_target_pairs={{0,1},{1,0},{2,3},{3,2},{4,5},{5,4},{6,7},{7,6},{8,9},{9,8},{10,11... | collective-permute-start | bytes 884744 | tf_op jit(solution)/shard_map/ppermute | solution.py:172
  45.6 2.4 %collective-permute-start.7 = (bf16[8,144,128]{2,1,0:T(8,128)(2,1)S(1)}, bf16[8,144,128]{2,1,0:T(8,128)(2,1)S(1)}, u32[]{:S(2)}, u32[]{:S(2)}) collective-permute-start(bf16[8,144,128]{2,1,0:T(8,128)(2,1)S(1)} %collective-permute-done.5.mine_b), channel_id=1, source_target_pairs={{0,1},{1,0},{2,3},{3,2},{4,5},{5,4},{6,7},{7,6},{8,9},{9,8},{10,11... | collective-permute-start | bytes 884744 | tf_op jit(solution)/shard_map/ppermute | solution.py:172
  48.0 1.9 %collective-permute-start.1 = (bf16[2,256,256]{2,1,0:T(8,128)(2,1)S(1)}, bf16[2,256,256]{2,1,0:T(8,128)(2,1)S(1)}, u32[]{:S(2)}, u32[]{:S(2)}) collective-permute-start(bf16[2,256,256]{2,1,0:T(8,128)(2,1)S(1)} %bitcast.18), channel_id=1, source_target_pairs={{1,2},{2,1},{3,4},{4,3},{5,6},{6,5},{7,8},{8,7},{9,10},{10,9},{11,... | collective-permute-start | bytes 786440 | tf_op jit(solution)/shard_map/ppermute | solution.py:171
  50.0 1.9 %collective-permute-start.9 = (bf16[8,144,128]{2,1,0:T(8,128)(2,1)S(1)}, bf16[8,144,128]{2,1,0:T(8,128)(2,1)S(1)}, u32[]{:S(2)}, u32[]{:S(2)}) collective-permute-start(bf16[8,144,128]{2,1,0:T(8,128)(2,1)S(1)} %get-tuple-element.6.mine_a), channel_id=1, source_target_pairs={{0,1},{1,0},{2,3},{3,2},{4,5},{5,4},{6,7},{7,6},{8,9},{9,8},{10,11... | collective-permute-start | bytes 884744 | tf_op jit(solution)/shard_map/ppermute | solution.py:172
  51.9 2.4 %collective-permute-start.10 = (bf16[8,144,128]{2,1,0:T(8,128)(2,1)S(1)}, bf16[8,144,128]{2,1,0:T(8,128)(2,1)S(1)}, u32[]{:S(2)}, u32[]{:S(2)}) collective-permute-start(bf16[8,144,128]{2,1,0:T(8,128)(2,1)S(1)} %collective-permute-done.8.mine_b), channel_id=1, source_target_pairs={{0,1},{1,0},{2,3},{3,2},{4,5},{5,4},{6,7},{7,6},{8,9},{9,8},{10,11... | collective-permute-start | bytes 884744 | tf_op jit(solution)/shard_map/ppermute | solution.py:172
  55.0 4.7 %collective-permute-done.1.far = bf16[2,256,256]{2,1,0:T(8,128)(2,1)S(1)} collective-permute-done((bf16[2,256,256]{2,1,0:T(8,128)(2,1)S(1)}, bf16[2,256,256]{2,1,0:T(8,128)(2,1)S(1)}, u32[]{:S(2)}, u32[]{:S(2)}) %collective-permute-start.1) | collective-permute-done | bytes 262176 | tf_op jit(solution)/shard_map/ppermute | solution.py:171
  60.5 0.7 copy-done.6
  61.3 4.3 %first.1.inner = bf16[4,256,256]{2,1,0:T(8,128)(2,1)} custom-call(s32[1]{0:T(128)S(6)} %copy.10.ident, f32[16,256]{1,0:T(8,128)} %gains.3, bf16[2,256,256]{2,1,0:T(8,128)(2,1)} %bitcast.15, bf16[2,256,256]{2,1,0:T(8,128)(2,1)} %copy-done.10, bf16[2,256,256]{2,1,0:T(8,128)(2,1)} %copy-done.11, bf16[8,144,128]{2,1,0:T(8,128)(2,1)} %copy-done.2, ...), custom_call_target="tpu_custom_call" | custom-call | flops 1207959552 | bytes 4194304 | tf_op jit(solution)/shard_map/first/pallas_call | solution.py:174
  65.6 0.7 copy-done.7
  66.4 3.2 %second.1 = bf16[16,8,512]{2,1,0:T(8,128)(2,1)} custom-call(s32[1]{0:T(128)S(6)} %copy.10.ident, f32[16,256]{1,0:T(8,128)} %gains.3, bf16[2,256,256]{2,1,0:T(8,128)(2,1)} %bitcast.16, bf16[4,256,256]{2,1,0:T(8,128)(2,1)} %first.1.inner, bf16[8,256]{1,0:T(8,128)(2,1)} %bitcast.19, bf16[8,144,128]{2,1,0:T(8,128)(2,1)} %copy-done.1, ...), custom_call_target="tpu_custom_call" | custom-call | flops 603979776 | bytes 3145728 | tf_op jit(solution)/shard_map/second/pallas_call | solution.py:188
  69.6 4.8 %all-to-all-start = ((bf16[16,8,512]{2,1,0:T(8,128)(2,1)}), bf16[16,8,512]{2,1,0:T(8,128)(2,1)S(1)}, u32[]{:S(2)}, u32[]{:S(2)}) async-start(bf16[16,8,512]{2,1,0:T(8,128)(2,1)} %second.1), calls=%async_computation | async-start | bytes 262144 | tf_op jit(solution)/shard_map/all_to_all | solution.py:202
  77.0 4.7 %all-to-all-done.fields = bf16[16,8,512]{2,1,0:T(8,128)(2,1)S(1)} async-done(((bf16[16,8,512]{2,1,0:T(8,128)(2,1)}), bf16[16,8,512]{2,1,0:T(8,128)(2,1)S(1)}, u32[]{:S(2)}, u32[]{:S(2)}) %all-to-all-start) | async-done | bytes 131104 | tf_op jit(solution)/shard_map/all_to_all | solution.py:202
  82.3 1.9 %score.1 = (f32[8,2,256]{2,1,0:T(2,128)}, f32[32,1,128]{2,1,0:T(1,128)}) custom-call(f32[2]{0:T(128)} %dynamic-slice_divide_fusion.weight, bf16[16,8,512]{2,1,0:T(8,128)(2,1)} %copy-done, f32[8,2,256]{2,1,0:T(2,128)} %target.1), custom_call_target="tpu_custom_call" | custom-call | tf_op jit(solution)/shard_map/score/pallas_call | solution.py:211
  84.2 28.5 %all_to_all.10 = f32[32,1,128]{2,1,0:T(1,128)S(1)} all-to-all(f32[32,1,128]{2,1,0:T(1,128)} %get-tuple-element.5), channel_id=1, replica_groups=mesh['member'=16,'lat'=32] {'lat'}, dimensions={0} | all-to-all | bytes 32768 | tf_op jit(solution)/shard_map/all_to_all | solution.py:221
  (37 shorter events, 3.7 us)
Async XLA Ops:
  1.5 7.7 %collective-permute-start.2 = (bf16[1,2,144,128]{3,2,0,1:T(8,128)(2,1)S(1)}, bf16[1,2,144,128]{3,2,0,1:T(8,128)(2,1)S(1)}, u32[]{:S(2)}, u32[]{:S(2)}) collective-permute-start(bf16[1,2,144,128]{3,2,0,1:T(8,128)(2,1)S(1)} %fusion.2), channel_id=1, source_target_pairs={{0,32},{1,99},{2,34},{3,97},{4,36},{5,103},{6,38},{7,101},{8,40},{... | collective-permute-start | bytes 221192 | tf_op jit(solution)/shard_map/ppermute | solution.py:36
  9.2 6.3 %collective-permute-start.3 = (bf16[2,2,144,128]{3,2,0,1:T(8,128)(2,1)S(1)}, bf16[2,2,144,128]{3,2,0,1:T(8,128)(2,1)S(1)}, u32[]{:S(2)}, u32[]{:S(2)}) collective-permute-start(bf16[2,2,144,128]{3,2,0,1:T(8,128)(2,1)S(1)} %pad_maximum_fusion.2), channel_id=1, source_target_pairs={{0,98},{1,33},{2,96},{3,35},{4,102},{5,37},{6,100},{7,39},{8,106},... | collective-permute-start | bytes 442376 | tf_op jit(solution)/shard_map/ppermute | solution.py:36
  15.5 8.7 %collective-permute-start.4 = (bf16[4,2,144,128]{3,2,0,1:T(8,128)(2,1)S(1)}, bf16[4,2,144,128]{3,2,0,1:T(8,128)(2,1)S(1)}, u32[]{:S(2)}, u32[]{:S(2)}) collective-permute-start(bf16[4,2,144,128]{3,2,0,1:T(8,128)(2,1)S(1)} %pad_maximum_fusion.1), channel_id=1, source_target_pairs={{0,128},{1,385},{2,130},{3,387},{4,132},{5,389},{6,134},{7,391},{8... | collective-permute-start | bytes 884744 | tf_op jit(solution)/shard_map/ppermute | solution.py:36
  24.2 5.4 %copy-start.9 = (bf16[1,2,256,256]{3,2,1,0:T(8,128)(2,1)S(1)}, bf16[1,2,256,256]{3,2,1,0:T(8,128)(2,1)}, u32[]{:S(2)}) copy-start(bf16[1,2,256,256]{3,2,1,0:T(8,128)(2,1)} %param.8) | copy-start | bytes 786436
  24.3 35.4 %copy-start.2 = (bf16[8,144,128]{2,1,0:T(8,128)(2,1)}, bf16[8,144,128]{2,1,0:T(8,128)(2,1)S(1)}, u32[]{:S(2)}) copy-start(bf16[8,144,128]{2,1,0:T(8,128)(2,1)S(1)} %get-tuple-element.7.mine_a) | copy-start | bytes 884740
  24.3 41.2 %copy-start.1 = (bf16[8,144,128]{2,1,0:T(8,128)(2,1)}, bf16[8,144,128]{2,1,0:T(8,128)(2,1)S(1)}, u32[]{:S(2)}) copy-start(bf16[8,144,128]{2,1,0:T(8,128)(2,1)S(1)} %get-tuple-element.6.mine_a) | copy-start | bytes 884740
  24.3 21.2 %collective-permute-start.5 = (bf16[8,144,128]{2,1,0:T(8,128)(2,1)S(1)}, bf16[8,144,128]{2,1,0:T(8,128)(2,1)S(1)}, u32[]{:S(2)}, u32[]{:S(2)}) collective-permute-start(bf16[8,144,128]{2,1,0:T(8,128)(2,1)S(1)} %get-tuple-element.7.mine_a), channel_id=1, source_target_pairs={{0,384},{1,129},{2,386},{3,131},{4,388},{5,133},{6,390},{7,135},{8... | collective-permute-start | bytes 884744 | tf_op jit(solution)/shard_map/ppermute | solution.py:36
  26.3 25.6 %collective-permute-start.8 = (bf16[8,144,128]{2,1,0:T(8,128)(2,1)S(1)}, bf16[8,144,128]{2,1,0:T(8,128)(2,1)S(1)}, u32[]{:S(2)}, u32[]{:S(2)}) collective-permute-start(bf16[8,144,128]{2,1,0:T(8,128)(2,1)S(1)} %get-tuple-element.6.mine_a), channel_id=1, source_target_pairs={{0,384},{1,129},{2,386},{3,131},{4,388},{5,133},{6,390},{7,135},{8... | collective-permute-start | bytes 884744 | tf_op jit(solution)/shard_map/ppermute | solution.py:36
  29.6 20.3 %collective-permute-start = (bf16[2,256,256]{2,1,0:T(8,128)(2,1)S(1)}, bf16[2,256,256]{2,1,0:T(8,128)(2,1)S(1)}, u32[]{:S(2)}, u32[]{:S(2)}) collective-permute-start(bf16[2,256,256]{2,1,0:T(8,128)(2,1)S(1)} %bitcast.17), channel_id=1, source_target_pairs={{0,1},{1,0},{2,3},{3,2},{4,5},{5,4},{6,7},{7,6},{8,9},{9,8},{10,11... | collective-permute-start | bytes 786440 | tf_op jit(solution)/shard_map/ppermute | solution.py:170
  43.6 16.1 %collective-permute-start.6 = (bf16[8,144,128]{2,1,0:T(8,128)(2,1)S(1)}, bf16[8,144,128]{2,1,0:T(8,128)(2,1)S(1)}, u32[]{:S(2)}, u32[]{:S(2)}) collective-permute-start(bf16[8,144,128]{2,1,0:T(8,128)(2,1)S(1)} %get-tuple-element.7.mine_a), channel_id=1, source_target_pairs={{0,1},{1,0},{2,3},{3,2},{4,5},{5,4},{6,7},{7,6},{8,9},{9,8},{10,11... | collective-permute-start | bytes 884744 | tf_op jit(solution)/shard_map/ppermute | solution.py:172
  45.6 14.2 %copy-start.4 = (bf16[8,144,128]{2,1,0:T(8,128)(2,1)}, bf16[8,144,128]{2,1,0:T(8,128)(2,1)S(1)}, u32[]{:S(2)}) copy-start(bf16[8,144,128]{2,1,0:T(8,128)(2,1)S(1)} %collective-permute-done.5.mine_b) | copy-start | bytes 884740
  45.6 14.1 %collective-permute-start.7 = (bf16[8,144,128]{2,1,0:T(8,128)(2,1)S(1)}, bf16[8,144,128]{2,1,0:T(8,128)(2,1)S(1)}, u32[]{:S(2)}, u32[]{:S(2)}) collective-permute-start(bf16[8,144,128]{2,1,0:T(8,128)(2,1)S(1)} %collective-permute-done.5.mine_b), channel_id=1, source_target_pairs={{0,1},{1,0},{2,3},{3,2},{4,5},{5,4},{6,7},{7,6},{8,9},{9,8},{10,11... | collective-permute-start | bytes 884744 | tf_op jit(solution)/shard_map/ppermute | solution.py:172
  48.0 11.7 %collective-permute-start.1 = (bf16[2,256,256]{2,1,0:T(8,128)(2,1)S(1)}, bf16[2,256,256]{2,1,0:T(8,128)(2,1)S(1)}, u32[]{:S(2)}, u32[]{:S(2)}) collective-permute-start(bf16[2,256,256]{2,1,0:T(8,128)(2,1)S(1)} %bitcast.18), channel_id=1, source_target_pairs={{1,2},{2,1},{3,4},{4,3},{5,6},{6,5},{7,8},{8,7},{9,10},{10,9},{11,... | collective-permute-start | bytes 786440 | tf_op jit(solution)/shard_map/ppermute | solution.py:171
  49.9 9.8 %copy-start.10 = (bf16[2,256,256]{2,1,0:T(8,128)(2,1)}, bf16[2,256,256]{2,1,0:T(8,128)(2,1)S(1)}, u32[]{:S(2)}) copy-start(bf16[2,256,256]{2,1,0:T(8,128)(2,1)S(1)} %collective-permute-done.near) | copy-start | bytes 786436
  50.0 15.6 %collective-permute-start.9 = (bf16[8,144,128]{2,1,0:T(8,128)(2,1)S(1)}, bf16[8,144,128]{2,1,0:T(8,128)(2,1)S(1)}, u32[]{:S(2)}, u32[]{:S(2)}) collective-permute-start(bf16[8,144,128]{2,1,0:T(8,128)(2,1)S(1)} %get-tuple-element.6.mine_a), channel_id=1, source_target_pairs={{0,1},{1,0},{2,3},{3,2},{4,5},{5,4},{6,7},{7,6},{8,9},{9,8},{10,11... | collective-permute-start | bytes 884744 | tf_op jit(solution)/shard_map/ppermute | solution.py:172
  51.9 13.6 %copy-start.3 = (bf16[8,144,128]{2,1,0:T(8,128)(2,1)}, bf16[8,144,128]{2,1,0:T(8,128)(2,1)S(1)}, u32[]{:S(2)}) copy-start(bf16[8,144,128]{2,1,0:T(8,128)(2,1)S(1)} %collective-permute-done.8.mine_b) | copy-start | bytes 884740
  51.9 13.6 %collective-permute-start.10 = (bf16[8,144,128]{2,1,0:T(8,128)(2,1)S(1)}, bf16[8,144,128]{2,1,0:T(8,128)(2,1)S(1)}, u32[]{:S(2)}, u32[]{:S(2)}) collective-permute-start(bf16[8,144,128]{2,1,0:T(8,128)(2,1)S(1)} %collective-permute-done.8.mine_b), channel_id=1, source_target_pairs={{0,1},{1,0},{2,3},{3,2},{4,5},{5,4},{6,7},{7,6},{8,9},{9,8},{10,11... | collective-permute-start | bytes 884744 | tf_op jit(solution)/shard_map/ppermute | solution.py:172
  59.7 0.7 copy-start.11
  59.7 0.8 copy-start.5
  60.5 0.7 copy-start.6
  65.5 0.7 copy-start.7
  65.6 0.8 copy-start.8
  69.6 12.1 %all-to-all-start = ((bf16[16,8,512]{2,1,0:T(8,128)(2,1)}), bf16[16,8,512]{2,1,0:T(8,128)(2,1)S(1)}, u32[]{:S(2)}, u32[]{:S(2)}) async-start(bf16[16,8,512]{2,1,0:T(8,128)(2,1)} %second.1), calls=%async_computation | async-start | bytes 262144 | tf_op jit(solution)/shard_map/all_to_all | solution.py:202
  81.6 0.6 copy-start

commit v2 on v1

--- a/solution.py
+++ b/solution.py
@@ -9,10 +9,11 @@
 
 MEMBERS, BANDS = 16, 32
 AXES = ("member", "lat")
+LIMIT = 20 << 20
 
 
 def partner_in_y(member, lat, flip):
-    low, high = member % 4, lat // 2 % 2
+    low = member % 4
     if flip == 1:
         return member ^ 1, lat
     return member ^ 3, lat ^ 2 if low in (0, 3) else lat
@@ -34,6 +35,15 @@
 
 def swap(block, partner, step):
     return lax.ppermute(block, AXES, pairing(partner, step))
+
+
+def mean_groups():
+    groups = []
+    for member in range(MEMBERS):
+        groups.append(
+            [(member ^ 2 * (lat // 2 % 2)) * BANDS + lat for lat in range(BANDS)]
+        )
+    return groups
 
 
 def tap_sum(shifted, weights, first, rows):
@@ -61,7 +71,8 @@
     shifted[2, row] = after.astype(jnp.bfloat16)
 
 
-def put_weights(weights, core, member, blocks, depth):
+def put_weights(weights, core, member, blocks, which):
+    depth = blocks[0].shape[2]
     turns = jnp.where(core == 0, 1, 3)
     masks = (0, turns, turns ^ 2, 2)
     at = 0
@@ -69,7 +80,8 @@
         for index in range(ref.shape[0]):
             mask = masks[at // 4] * 4 + masks[at % 4]
             origin = (member ^ mask) * depth
-            weights[core, pl.ds(pl.multiple_of(origin, 16), depth), :] = ref[index]
+            block = ref[index] if len(ref.shape) == 3 else ref[index, which]
+            weights[core, pl.ds(pl.multiple_of(origin, 16), depth), :] = block
             at += 1
 
 
@@ -78,15 +90,14 @@
 ):
     member, lat = lax.axis_index("member"), lax.axis_index("lat")
     core = lat % 2
-    depth = mine_a.shape[1]
     gain = gains[pl.ds(ident[0], 1), :]
     rows = own.shape[0]
     for ref, base in ((own, rows), (near, 2 * rows * (1 - core)), (far, 2 * rows * core)):
         for row in range(rows):
             value = (ref[row].astype(jnp.float32) * gain).astype(jnp.bfloat16)
             put_shifted(shifted, base + row, value.astype(jnp.float32))
-    put_weights(weights, core, member, (mine_a, mine_b), depth)
-    put_weights(weights, 1 - core, member, (other_a, other_b), depth)
+    put_weights(weights, core, member, (mine_a, mine_b), 0)
+    put_weights(weights, 1 - core, member, (other_a, other_b), 0)
     for half in range(2):
         out = tap_sum(shifted, weights, 2 * half, 2)
         out = jax.nn.gelu(out, approximate=True)
@@ -105,12 +116,11 @@
 ):
     member, lat = lax.axis_index("member"), lax.axis_index("lat")
     core = lat % 2
-    depth = mine_a.shape[1]
     gain = gains[pl.ds(ident[0], 1), :]
     for row in range(inner.shape[0]):
         put_shifted(shifted, row, inner[row].astype(jnp.float32))
-    put_weights(weights, core, member, (mine_a, mine_b), depth)
-    put_weights(weights, 1 - core, member, (other_a, other_b), depth)
+    put_weights(weights, core, member, (mine_a, mine_b), 1)
+    put_weights(weights, 1 - core, member, (other_a, other_b), 1)
     rows, cols, chans = own.shape
     out = tap_sum(shifted, weights, 0, rows)
     start = (own[...].reshape(rows * cols, chans).astype(jnp.float32) * gain).astype(jnp.bfloat16)
@@ -150,7 +160,6 @@
 
 def body(states, member_id, member_gain, first_conv, second_conv, head, target, lat_start):
     rows, cols, chans = (states.shape[1], states.shape[2], states.shape[3])
-    depth = first_conv.shape[0]
     lat = lax.axis_index("lat")
     core = lat % 2
     own = states[0]
@@ -169,7 +178,9 @@
     across = [(lat_id, ((lat_id + 1) ^ 1) - 1) for lat_id in range(1, BANDS - 1)]
     near = lax.ppermute(own, "lat", on_chip)
     far = lax.ppermute(own, "lat", across)
-    others = [lax.ppermute(block, "lat", on_chip) for block in (first_a, first_b, second_a, second_b)]
+    other = lax.ppermute(mine, "lat", on_chip)
+    first_o = lax.ppermute(first_b, "lat", on_chip)
+    second_o = lax.ppermute(second_b, "lat", on_chip)
 
     inner = pl.pallas_call(
         first_kernel,
@@ -183,8 +194,9 @@
         cost_estimate=pl.CostEstimate(
             flops=2 * (rows + 2) * cols * 9 * chans * chans, bytes_accessed=4 << 20, transcendentals=0
         ),
+        compiler_params=pltpu.CompilerParams(vmem_limit_bytes=LIMIT),
         name="first",
-    )(member_id, member_gain, own, near, far, first_a, first_b, others[0], others[1])
+    )(member_id, member_gain, own, near, far, mine, first_b, other, first_o)
     pred = pl.pallas_call(
         second_kernel,
         out_shape=jax.ShapeDtypeStruct((MEMBERS, head.shape[1], rows * cols), jnp.bfloat16),
@@ -197,8 +209,9 @@
         cost_estimate=pl.CostEstimate(
             flops=2 * rows * cols * 9 * chans * chans, bytes_accessed=3 << 20, transcendentals=0
         ),
+        compiler_params=pltpu.CompilerParams(vmem_limit_bytes=LIMIT),
         name="second",
-    )(member_id, member_gain, own, inner, head.T, second_a, second_b, others[2], others[3])
+    )(member_id, member_gain, own, inner, head.T, mine, second_b, other, second_o)
     fields = lax.all_to_all(pred, "member", 0, 0, tiled=True)
 
     row_ids = lat_start[0] + jnp.arange(BANDS * rows, dtype=jnp.int32)
@@ -216,9 +229,12 @@
         ),
         in_specs=[SMEM, VMEM, VMEM],
         out_specs=(VMEM, VMEM),
+        compiler_params=pltpu.CompilerParams(vmem_limit_bytes=LIMIT),
         name="score",
     )(weight, fields, target)
-    shares = lax.all_to_all(partial, "lat", 0, 0, tiled=True)
+    shares = lax.all_to_all(
+        partial, AXES, 0, 0, axis_index_groups=mean_groups(), tiled=True
+    )
     return (score, jnp.sum(shares[:, 0, 0]))
 
 
@@ -234,6 +250,7 @@
         P(None, "lat", None),
         P(),
     )
+
     return jax.shard_map(
         body, mesh=mesh, in_specs=placed, out_specs=(P(None, "lat", None), P()), check_vma=False
     )

time: 114 us -> 105 us (0.921)
  waiting for transfers between devices: 20.2 us -> 27.1 us
  starting transfers between devices: 46.5 us -> 42 us
  Pallas kernels: 9.35 us -> 5.11 us
  blocking collectives: 28.5 us -> 25.3 us
  local copies, waits for them, and re-layouts: 3.04 us -> 0.14 us
    ppermute x1, starting transfers between devices: 14 us -> 1.92 us  [body(): near = lax.ppermute(own, 'lat', on_chip)]
    ppermute x4 -> x3, starting transfers between devices: 8.65 us -> 15.7 us  [the longest x1 9.77 us: body(): other = lax.ppermute(mine, 'lat', on_chip)]
    ppermute x1, waiting for transfers between devices: 4.74 us -> 8.62 us  [body(): far = lax.ppermute(own, 'lat', across)]
    all_to_all x1, blocking collectives: 28.5 us -> 25.3 us  [body(): lax.all_to_all(partial, AXES, 0, 0, axis_index_groups=mean_groups(), tile...]
    unnamed x24 -> x8, local copies, waits for them, and re-layouts: 3 us -> 0.02 us
    ppermute x5, waiting for transfers between devices: 10.8 us -> 13.3 us  [swap(): return lax.ppermute(block, AXES, pairing(partner, step))]
    pallas_call x1, Pallas kernels: 4.26 us -> 1.99 us  [body(): pl.pallas_call(first_kernel, out_shape=jax.ShapeDtypeStruct((rows + 2, co...]
    pallas_call x1, Pallas kernels: 3.21 us -> 1.73 us  [body(): pl.pallas_call(second_kernel, out_shape=jax.ShapeDtypeStruct((MEMBERS, he...]
  transfers between devices with their start and end apart: 12 -> 11, of which waited for: 5 -> 6; matrix products, arithmetic and copies ran while one was open for 1% -> 1% of each run, Pallas kernels for 4% -> 2%
where the time goes in v2:
time: 105 us
  starting transfers between devices  42 us (40%)
  waiting for transfers between devices  27.1 us (26%)
  blocking collectives  25.3 us (24%)
  Pallas kernels  5.11 us (5%)
  between operations  2.81 us (3%)
  other arithmetic  2.36 us (2%)
    all_to_all x1, blocking collectives, body(): lax.all_to_all(partial, AXES, 0, 0, axis_index_groups=mean_groups(), tile...  25.3 us
    ppermute x5, starting transfers between devices, swap(): return lax.ppermute(block, AXES, pairing(partner, step))  17.1 us
    ppermute x5, waiting for transfers between devices, swap(): return lax.ppermute(block, AXES, pairing(partner, step))  13.3 us
    ppermute x1, starting transfers between devices, body(): other = lax.ppermute(mine, 'lat', on_chip)  9.77 us
    ppermute x1, waiting for transfers between devices, body(): far = lax.ppermute(own, 'lat', across)  8.62 us
    all_to_all x1, starting transfers between devices, body(): fields = lax.all_to_all(pred, 'member', 0, 0, tiled=True)  5.23 us
    all_to_all x1, waiting for transfers between devices, body(): fields = lax.all_to_all(pred, 'member', 0, 0, tiled=True)  5.15 us
    ppermute x1, starting transfers between devices, body(): first_o = lax.ppermute(first_b, 'lat', on_chip)  3.97 us
  transfers between devices with their start and end apart: 11, of which 6 were waited for; matrix products, arithmetic and copies ran while one was open for 1% of the time, Pallas kernels for 2%

profile of v2, /device:TPU:1, one launch (start us, length us, event | category | flops | bytes accessed | tf_op | source)
XLA Modules:
  0.0 104.8 jit_solution(10999794627850307397)
XLA Ops:
  0.6 0.8 fusion.2
  1.5 5.9 %collective-permute-start.2 = (bf16[1,2,144,128]{3,2,0,1:T(8,128)(2,1)S(1)}, bf16[1,2,144,128]{3,2,0,1:T(8,128)(2,1)S(1)}, u32[]{:S(2)}, u32[]{:S(2)}) collective-permute-start(bf16[1,2,144,128]{3,2,0,1:T(8,128)(2,1)S(1)} %fusion.2), channel_id=1, source_target_pairs={{0,32},{1,99},{2,34},{3,97},{4,36},{5,103},{6,38},{7,101},{8,40},{... | collective-permute-start | bytes 221192 | tf_op jit(solution)/shard_map/ppermute | solution.py:37
  7.4 1.7 %collective-permute-done.2 = bf16[1,2,144,128]{3,2,0,1:T(8,128)(2,1)S(1)} collective-permute-done((bf16[1,2,144,128]{3,2,0,1:T(8,128)(2,1)S(1)}, bf16[1,2,144,128]{3,2,0,1:T(8,128)(2,1)S(1)}, u32[]{:S(2)}, u32[]{:S(2)}) %collective-permute-start.2) | collective-permute-done | bytes 73760 | tf_op jit(solution)/shard_map/ppermute | solution.py:37
  9.2 1.9 %collective-permute-start.3 = (bf16[2,2,144,128]{3,2,0,1:T(8,128)(2,1)S(1)}, bf16[2,2,144,128]{3,2,0,1:T(8,128)(2,1)S(1)}, u32[]{:S(2)}, u32[]{:S(2)}) collective-permute-start(bf16[2,2,144,128]{3,2,0,1:T(8,128)(2,1)S(1)} %pad_maximum_fusion.2), channel_id=1, source_target_pairs={{0,98},{1,33},{2,96},{3,35},{4,102},{5,37},{6,100},{7,39},{8,106},... | collective-permute-start | bytes 442376 | tf_op jit(solution)/shard_map/ppermute | solution.py:37
  11.1 4.4 %collective-permute-done.3 = bf16[2,2,144,128]{3,2,0,1:T(8,128)(2,1)S(1)} collective-permute-done((bf16[2,2,144,128]{3,2,0,1:T(8,128)(2,1)S(1)}, bf16[2,2,144,128]{3,2,0,1:T(8,128)(2,1)S(1)}, u32[]{:S(2)}, u32[]{:S(2)}) %collective-permute-start.3) | collective-permute-done | bytes 147488 | tf_op jit(solution)/shard_map/ppermute | solution.py:37
  15.5 4.0 %collective-permute-start.4 = (bf16[4,2,144,128]{3,2,0,1:T(8,128)(2,1)S(1)}, bf16[4,2,144,128]{3,2,0,1:T(8,128)(2,1)S(1)}, u32[]{:S(2)}, u32[]{:S(2)}) collective-permute-start(bf16[4,2,144,128]{3,2,0,1:T(8,128)(2,1)S(1)} %pad_maximum_fusion.1), channel_id=1, source_target_pairs={{0,128},{1,385},{2,130},{3,387},{4,132},{5,389},{6,134},{7,391},{8... | collective-permute-start | bytes 884744 | tf_op jit(solution)/shard_map/ppermute | solution.py:37
  19.5 4.7 %collective-permute-done.4 = bf16[4,2,144,128]{3,2,0,1:T(8,128)(2,1)S(1)} collective-permute-done((bf16[4,2,144,128]{3,2,0,1:T(8,128)(2,1)S(1)}, bf16[4,2,144,128]{3,2,0,1:T(8,128)(2,1)S(1)}, u32[]{:S(2)}, u32[]{:S(2)}) %collective-permute-start.4) | collective-permute-done | bytes 294944 | tf_op jit(solution)/shard_map/ppermute | solution.py:37
  24.3 9.8 %collective-permute-start.6 = (bf16[8,2,144,128]{3,2,0,1:T(8,128)(2,1)S(1)}, bf16[8,2,144,128]{3,2,0,1:T(8,128)(2,1)S(1)}, u32[]{:S(2)}, u32[]{:S(2)}) collective-permute-start(bf16[8,2,144,128]{3,2,0,1:T(8,128)(2,1)S(1)} %pad_maximum_fusion), channel_id=1, source_target_pairs={{0,1},{1,0},{2,3},{3,2},{4,5},{5,4},{6,7},{7,6},{8,9},{9,8},{10,11... | collective-permute-start | bytes 1769480 | tf_op jit(solution)/shard_map/ppermute | solution.py:181
  34.1 1.9 %collective-permute-start.5 = (bf16[8,144,128]{2,1,0:T(8,128)(2,1)S(1)}, bf16[8,144,128]{2,1,0:T(8,128)(2,1)S(1)}, u32[]{:S(2)}, u32[]{:S(2)}) collective-permute-start(bf16[8,144,128]{2,1,0:T(8,128)(2,1)S(1)} %get-tuple-element.7), channel_id=1, source_target_pairs={{0,384},{1,129},{2,386},{3,131},{4,388},{5,133},{6,390},{7,135},{8... | collective-permute-start | bytes 884744 | tf_op jit(solution)/shard_map/ppermute | solution.py:37
  36.0 3.4 %collective-permute-start.8 = (bf16[8,144,128]{2,1,0:T(8,128)(2,1)S(1)}, bf16[8,144,128]{2,1,0:T(8,128)(2,1)S(1)}, u32[]{:S(2)}, u32[]{:S(2)}) collective-permute-start(bf16[8,144,128]{2,1,0:T(8,128)(2,1)S(1)} %get-tuple-element.6), channel_id=1, source_target_pairs={{0,384},{1,129},{2,386},{3,131},{4,388},{5,133},{6,390},{7,135},{8... | collective-permute-start | bytes 884744 | tf_op jit(solution)/shard_map/ppermute | solution.py:37
  39.4 2.5 %collective-permute-done.5.mine_b = bf16[8,144,128]{2,1,0:T(8,128)(2,1)S(1)} collective-permute-done((bf16[8,144,128]{2,1,0:T(8,128)(2,1)S(1)}, bf16[8,144,128]{2,1,0:T(8,128)(2,1)S(1)}, u32[]{:S(2)}, u32[]{:S(2)}) %collective-permute-start.5) | collective-permute-done | bytes 294944 | tf_op jit(solution)/shard_map/ppermute | solution.py:37
  41.9 4.0 %collective-permute-start.7 = (bf16[8,144,128]{2,1,0:T(8,128)(2,1)S(1)}, bf16[8,144,128]{2,1,0:T(8,128)(2,1)S(1)}, u32[]{:S(2)}, u32[]{:S(2)}) collective-permute-start(bf16[8,144,128]{2,1,0:T(8,128)(2,1)S(1)} %collective-permute-done.5.mine_b), channel_id=1, source_target_pairs={{0,1},{1,0},{2,3},{3,2},{4,5},{5,4},{6,7},{7,6},{8,9},{9,8},{10,11... | collective-permute-start | bytes 884744 | tf_op jit(solution)/shard_map/ppermute | solution.py:182
  45.8 1.9 %collective-permute-start = (bf16[2,256,256]{2,1,0:T(8,128)(2,1)S(1)}, bf16[2,256,256]{2,1,0:T(8,128)(2,1)S(1)}, u32[]{:S(2)}, u32[]{:S(2)}) collective-permute-start(bf16[2,256,256]{2,1,0:T(8,128)(2,1)S(1)} %bitcast.13), channel_id=1, source_target_pairs={{0,1},{1,0},{2,3},{3,2},{4,5},{5,4},{6,7},{7,6},{8,9},{9,8},{10,11... | collective-permute-start | bytes 786440 | tf_op jit(solution)/shard_map/ppermute | solution.py:179
  47.8 2.1 %collective-permute-start.1 = (bf16[2,256,256]{2,1,0:T(8,128)(2,1)S(1)}, bf16[2,256,256]{2,1,0:T(8,128)(2,1)S(1)}, u32[]{:S(2)}, u32[]{:S(2)}) collective-permute-start(bf16[2,256,256]{2,1,0:T(8,128)(2,1)S(1)} %bitcast.14), channel_id=1, source_target_pairs={{1,2},{2,1},{3,4},{4,3},{5,6},{6,5},{7,8},{8,7},{9,10},{10,9},{11,... | collective-permute-start | bytes 786440 | tf_op jit(solution)/shard_map/ppermute | solution.py:180
  49.9 1.9 %collective-permute-start.9 = (bf16[8,144,128]{2,1,0:T(8,128)(2,1)S(1)}, bf16[8,144,128]{2,1,0:T(8,128)(2,1)S(1)}, u32[]{:S(2)}, u32[]{:S(2)}) collective-permute-start(bf16[8,144,128]{2,1,0:T(8,128)(2,1)S(1)} %collective-permute-done.8.mine_b), channel_id=1, source_target_pairs={{0,1},{1,0},{2,3},{3,2},{4,5},{5,4},{6,7},{7,6},{8,9},{9,8},{10,11... | collective-permute-start | bytes 884744 | tf_op jit(solution)/shard_map/ppermute | solution.py:183
  52.6 8.6 %collective-permute-done.1.far = bf16[2,256,256]{2,1,0:T(8,128)(2,1)S(1)} collective-permute-done((bf16[2,256,256]{2,1,0:T(8,128)(2,1)S(1)}, bf16[2,256,256]{2,1,0:T(8,128)(2,1)S(1)}, u32[]{:S(2)}, u32[]{:S(2)}) %collective-permute-start.1) | collective-permute-done | bytes 262176 | tf_op jit(solution)/shard_map/ppermute | solution.py:180
  61.2 2.0 %first.1.inner = bf16[4,256,256]{2,1,0:T(8,128)(2,1)S(1)} custom-call(s32[1]{0:T(128)S(6)} %copy.14.ident, f32[16,256]{1,0:T(8,128)S(1)} %copy-done.1, bf16[2,256,256]{2,1,0:T(8,128)(2,1)S(1)} %bitcast.15, bf16[2,256,256]{2,1,0:T(8,128)(2,1)S(1)} %collective-permute-done.near, bf16[2,256,256]{2,1,0:T(8,128)(2,1)S(1)} %collective-permute-done.1.far, ...), custom_call_target="tpu_custom_call" | custom-call | flops 1207959552 | bytes 4194304 | tf_op jit(solution)/shard_map/first/pallas_call | solution.py:185
  63.2 1.7 %second.1 = bf16[16,8,512]{2,1,0:T(8,128)(2,1)} custom-call(s32[1]{0:T(128)S(6)} %copy.14.ident, f32[16,256]{1,0:T(8,128)S(1)} %copy-done.1, bf16[2,256,256]{2,1,0:T(8,128)(2,1)S(1)} %bitcast.16, bf16[4,256,256]{2,1,0:T(8,128)(2,1)S(1)} %first.1.inner, bf16[8,256]{1,0:T(8,128)(2,1)S(1)} %bitcast.17, bf16[8,2,144,128]{3,2,1,0:T(8,128)(2,1)S(1)} %copy.10.mine_a, ...), custom_call_target="tpu_custom_call" | custom-call | flops 603979776 | bytes 3145728 | tf_op jit(solution)/shard_map/second/pallas_call | solution.py:200
  64.9 5.2 %all-to-all-start = ((bf16[16,8,512]{2,1,0:T(8,128)(2,1)}), bf16[16,8,512]{2,1,0:T(8,128)(2,1)S(1)}, u32[]{:S(2)}, u32[]{:S(2)}) async-start(bf16[16,8,512]{2,1,0:T(8,128)(2,1)} %second.1), calls=%async_computation | async-start | bytes 262144 | tf_op jit(solution)/shard_map/all_to_all | solution.py:215
  70.9 0.6 fusion.3
  72.3 5.2 %all-to-all-done.fields = bf16[16,8,512]{2,1,0:T(8,128)(2,1)S(1)} async-done(((bf16[16,8,512]{2,1,0:T(8,128)(2,1)}), bf16[16,8,512]{2,1,0:T(8,128)(2,1)S(1)}, u32[]{:S(2)}, u32[]{:S(2)}) %all-to-all-start) | async-done | bytes 131104 | tf_op jit(solution)/shard_map/all_to_all | solution.py:215
  77.4 1.4 %score.1 = (f32[8,2,256]{2,1,0:T(2,128)}, f32[32,1,128]{2,1,0:T(1,128)S(1)}) custom-call(f32[2]{0:T(128)S(1)} %dynamic-slice_divide_fusion.weight, bf16[16,8,512]{2,1,0:T(8,128)(2,1)S(1)} %all-to-all-done.fields, f32[8,2,256]{2,1,0:T(2,128)S(1)} %copy-done.2), custom_call_target="tpu_custom_call" | custom-call | tf_op jit(solution)/shard_map/score/pallas_call | solution.py:224
  78.8 25.3 %all_to_all.10 = f32[32,1,128]{2,1,0:T(1,128)S(1)} all-to-all(f32[32,1,128]{2,1,0:T(1,128)S(1)} %get-tuple-element.5), channel_id=1, replica_groups={{0,1,66,67,4,5,70,71,8,9,74,75,12,13,78,79,16,17,82,83,20,21,86,87,24,2..., dimensions={0} | all-to-all | bytes 32768 | tf_op jit(solution)/shard_map/all_to_all | solution.py:235
  104.1 0.6 slice_reduce_fusion
  (21 shorter events, 0.4 us)
Async XLA Ops:
  1.5 7.7 %collective-permute-start.2 = (bf16[1,2,144,128]{3,2,0,1:T(8,128)(2,1)S(1)}, bf16[1,2,144,128]{3,2,0,1:T(8,128)(2,1)S(1)}, u32[]{:S(2)}, u32[]{:S(2)}) collective-permute-start(bf16[1,2,144,128]{3,2,0,1:T(8,128)(2,1)S(1)} %fusion.2), channel_id=1, source_target_pairs={{0,32},{1,99},{2,34},{3,97},{4,36},{5,103},{6,38},{7,101},{8,40},{... | collective-permute-start | bytes 221192 | tf_op jit(solution)/shard_map/ppermute | solution.py:37
  9.2 6.3 %collective-permute-start.3 = (bf16[2,2,144,128]{3,2,0,1:T(8,128)(2,1)S(1)}, bf16[2,2,144,128]{3,2,0,1:T(8,128)(2,1)S(1)}, u32[]{:S(2)}, u32[]{:S(2)}) collective-permute-start(bf16[2,2,144,128]{3,2,0,1:T(8,128)(2,1)S(1)} %pad_maximum_fusion.2), channel_id=1, source_target_pairs={{0,98},{1,33},{2,96},{3,35},{4,102},{5,37},{6,100},{7,39},{8,106},... | collective-permute-start | bytes 442376 | tf_op jit(solution)/shard_map/ppermute | solution.py:37
  15.5 8.7 %collective-permute-start.4 = (bf16[4,2,144,128]{3,2,0,1:T(8,128)(2,1)S(1)}, bf16[4,2,144,128]{3,2,0,1:T(8,128)(2,1)S(1)}, u32[]{:S(2)}, u32[]{:S(2)}) collective-permute-start(bf16[4,2,144,128]{3,2,0,1:T(8,128)(2,1)S(1)} %pad_maximum_fusion.1), channel_id=1, source_target_pairs={{0,128},{1,385},{2,130},{3,387},{4,132},{5,389},{6,134},{7,391},{8... | collective-permute-start | bytes 884744 | tf_op jit(solution)/shard_map/ppermute | solution.py:37
  24.2 21.6 %copy-start = (bf16[1,2,256,256]{3,2,1,0:T(8,128)(2,1)S(1)}, bf16[1,2,256,256]{3,2,1,0:T(8,128)(2,1)}, u32[]{:S(2)}) copy-start(bf16[1,2,256,256]{3,2,1,0:T(8,128)(2,1)} %param.8) | copy-start | bytes 786436
  24.3 28.2 %collective-permute-start.6 = (bf16[8,2,144,128]{3,2,0,1:T(8,128)(2,1)S(1)}, bf16[8,2,144,128]{3,2,0,1:T(8,128)(2,1)S(1)}, u32[]{:S(2)}, u32[]{:S(2)}) collective-permute-start(bf16[8,2,144,128]{3,2,0,1:T(8,128)(2,1)S(1)} %pad_maximum_fusion), channel_id=1, source_target_pairs={{0,1},{1,0},{2,3},{3,2},{4,5},{5,4},{6,7},{7,6},{8,9},{9,8},{10,11... | collective-permute-start | bytes 1769480 | tf_op jit(solution)/shard_map/ppermute | solution.py:181
  34.1 7.8 %collective-permute-start.5 = (bf16[8,144,128]{2,1,0:T(8,128)(2,1)S(1)}, bf16[8,144,128]{2,1,0:T(8,128)(2,1)S(1)}, u32[]{:S(2)}, u32[]{:S(2)}) collective-permute-start(bf16[8,144,128]{2,1,0:T(8,128)(2,1)S(1)} %get-tuple-element.7), channel_id=1, source_target_pairs={{0,384},{1,129},{2,386},{3,131},{4,388},{5,133},{6,390},{7,135},{8... | collective-permute-start | bytes 884744 | tf_op jit(solution)/shard_map/ppermute | solution.py:37
  36.0 13.8 %collective-permute-start.8 = (bf16[8,144,128]{2,1,0:T(8,128)(2,1)S(1)}, bf16[8,144,128]{2,1,0:T(8,128)(2,1)S(1)}, u32[]{:S(2)}, u32[]{:S(2)}) collective-permute-start(bf16[8,144,128]{2,1,0:T(8,128)(2,1)S(1)} %get-tuple-element.6), channel_id=1, source_target_pairs={{0,384},{1,129},{2,386},{3,131},{4,388},{5,133},{6,390},{7,135},{8... | collective-permute-start | bytes 884744 | tf_op jit(solution)/shard_map/ppermute | solution.py:37
  41.9 19.3 %collective-permute-start.7 = (bf16[8,144,128]{2,1,0:T(8,128)(2,1)S(1)}, bf16[8,144,128]{2,1,0:T(8,128)(2,1)S(1)}, u32[]{:S(2)}, u32[]{:S(2)}) collective-permute-start(bf16[8,144,128]{2,1,0:T(8,128)(2,1)S(1)} %collective-permute-done.5.mine_b), channel_id=1, source_target_pairs={{0,1},{1,0},{2,3},{3,2},{4,5},{5,4},{6,7},{7,6},{8,9},{9,8},{10,11... | collective-permute-start | bytes 884744 | tf_op jit(solution)/shard_map/ppermute | solution.py:182
  45.8 6.7 %collective-permute-start = (bf16[2,256,256]{2,1,0:T(8,128)(2,1)S(1)}, bf16[2,256,256]{2,1,0:T(8,128)(2,1)S(1)}, u32[]{:S(2)}, u32[]{:S(2)}) collective-permute-start(bf16[2,256,256]{2,1,0:T(8,128)(2,1)S(1)} %bitcast.13), channel_id=1, source_target_pairs={{0,1},{1,0},{2,3},{3,2},{4,5},{5,4},{6,7},{7,6},{8,9},{9,8},{10,11... | collective-permute-start | bytes 786440 | tf_op jit(solution)/shard_map/ppermute | solution.py:179
  47.8 13.4 %collective-permute-start.1 = (bf16[2,256,256]{2,1,0:T(8,128)(2,1)S(1)}, bf16[2,256,256]{2,1,0:T(8,128)(2,1)S(1)}, u32[]{:S(2)}, u32[]{:S(2)}) collective-permute-start(bf16[2,256,256]{2,1,0:T(8,128)(2,1)S(1)} %bitcast.14), channel_id=1, source_target_pairs={{1,2},{2,1},{3,4},{4,3},{5,6},{6,5},{7,8},{8,7},{9,10},{10,9},{11,... | collective-permute-start | bytes 786440 | tf_op jit(solution)/shard_map/ppermute | solution.py:180
  49.9 13.3 %collective-permute-start.9 = (bf16[8,144,128]{2,1,0:T(8,128)(2,1)S(1)}, bf16[8,144,128]{2,1,0:T(8,128)(2,1)S(1)}, u32[]{:S(2)}, u32[]{:S(2)}) collective-permute-start(bf16[8,144,128]{2,1,0:T(8,128)(2,1)S(1)} %collective-permute-done.8.mine_b), channel_id=1, source_target_pairs={{0,1},{1,0},{2,3},{3,2},{4,5},{5,4},{6,7},{7,6},{8,9},{9,8},{10,11... | collective-permute-start | bytes 884744 | tf_op jit(solution)/shard_map/ppermute | solution.py:183
  52.5 8.7 %copy-start.1 = (f32[16,256]{1,0:T(8,128)S(1)}, f32[16,256]{1,0:T(8,128)}, u32[]{:S(2)}) copy-start(f32[16,256]{1,0:T(8,128)} %gains.3) | copy-start | bytes 49156
  61.2 2.0 %copy-start.3 = (bf16[256,8]{0,1:T(8,128)(2,1)S(1)}, bf16[256,8]{0,1:T(8,128)(2,1)}, u32[]{:S(2)}) copy-start(bf16[256,8]{0,1:T(8,128)(2,1)} %param.13) | copy-start | bytes 12292
  64.9 12.5 %all-to-all-start = ((bf16[16,8,512]{2,1,0:T(8,128)(2,1)}), bf16[16,8,512]{2,1,0:T(8,128)(2,1)S(1)}, u32[]{:S(2)}, u32[]{:S(2)}) async-start(bf16[16,8,512]{2,1,0:T(8,128)(2,1)} %second.1), calls=%async_computation | async-start | bytes 262144 | tf_op jit(solution)/shard_map/all_to_all | solution.py:215
  70.2 7.3 %copy-start.2 = (f32[8,2,256]{2,1,0:T(2,128)S(1)}, f32[8,2,256]{2,1,0:T(2,128)}, u32[]{:S(2)}) copy-start(f32[8,2,256]{2,1,0:T(2,128)} %target.1) | copy-start | bytes 49156

commit v3 on v2

--- a/solution.py
+++ b/solution.py
@@ -35,6 +35,19 @@
 
 def swap(block, partner, step):
     return lax.ppermute(block, AXES, pairing(partner, step))
+
+
+def far_relays():
+    there, onward = [], []
+    for member in range(MEMBERS):
+        for lat in range(BANDS):
+            step = 1 if lat % 2 else -1
+            y = (lat // 2 % 2 * 4 + member % 4 + 2 * step) % 8
+            middle = (member // 4 * 4 + y % 4) * BANDS + lat // 4 * 4 + y // 4 * 2 + lat % 2
+            there.append((member * BANDS + lat, middle))
+            if 0 <= lat + step < BANDS:
+                onward.append((middle, member * BANDS + lat + step))
+    return there, onward
 
 
 def mean_groups():
@@ -77,10 +90,10 @@
     masks = (0, turns, turns ^ 2, 2)
     at = 0
     for ref in blocks:
-        for index in range(ref.shape[0]):
+        for index in range(ref.shape[-3]):
             mask = masks[at // 4] * 4 + masks[at % 4]
             origin = (member ^ mask) * depth
-            block = ref[index] if len(ref.shape) == 3 else ref[index, which]
+            block = ref[index] if len(ref.shape) == 3 else ref[which, index]
             weights[core, pl.ds(pl.multiple_of(origin, 16), depth), :] = block
             at += 1
 
@@ -166,18 +179,19 @@
 
     half = chans // 2
     shard = jnp.stack([first_conv, second_conv])
-    mine = jnp.where(core == 0, shard[:, :, :half], shard[:, :, half:])[None]
-    mine = jnp.concatenate([mine, swap(mine, partner_in_y, 0)], axis=0)
-    mine = jnp.concatenate([mine, swap(mine, partner_in_y, 1)], axis=0)
-    mine = jnp.concatenate([mine, swap(mine, partner_in_x, 0)], axis=0)
-    first_a, second_a = mine[:, 0], mine[:, 1]
+    mine = jnp.where(core == 0, shard[:, :, :half], shard[:, :, half:])[:, None]
+    mine = jnp.concatenate([mine, swap(mine, partner_in_y, 0)], axis=1)
+    mine = jnp.concatenate([mine, swap(mine, partner_in_y, 1)], axis=1)
+    mine = jnp.concatenate([mine, swap(mine, partner_in_x, 0)], axis=1)
+    first_a, second_a = mine[0], mine[1]
     first_b = swap(first_a, partner_in_x, 1)
     second_b = swap(second_a, partner_in_x, 1)
 
     on_chip = [(lat_id, lat_id ^ 1) for lat_id in range(BANDS)]
-    across = [(lat_id, ((lat_id + 1) ^ 1) - 1) for lat_id in range(1, BANDS - 1)]
     near = lax.ppermute(own, "lat", on_chip)
-    far = lax.ppermute(own, "lat", across)
+    there, onward = far_relays()
+    far = lax.ppermute(own, AXES, there)
+    far = lax.ppermute(far, AXES, onward)
     other = lax.ppermute(mine, "lat", on_chip)
     first_o = lax.ppermute(first_b, "lat", on_chip)
     second_o = lax.ppermute(second_b, "lat", on_chip)

time: 105 us -> 99.7 us (0.950)
  waiting for transfers between devices: 27.1 us -> 22.6 us
  blocking collectives: 25.3 us -> 23.4 us
    ppermute x1 -> x2, starting transfers between devices: 2.07 us -> 4.52 us  [the longest x1 2.6 us: body(): far = lax.ppermute(far, AXES, onward)]
    ppermute x1 -> x2, waiting for transfers between devices: 8.62 us -> 6.2 us  [the longest x1 6.19 us: body(): far = lax.ppermute(far, AXES, onward)]
    ppermute x5, waiting for transfers between devices: 13.3 us -> 11.3 us  [swap(): return lax.ppermute(block, AXES, pairing(partner, step))]
    all_to_all x1, blocking collectives: 25.3 us -> 23.4 us  [body(): lax.all_to_all(partial, AXES, 0, 0, axis_index_groups=mean_groups(), tile...]
    all_to_all x1, starting transfers between devices: 5.23 us -> 3.51 us  [body(): fields = lax.all_to_all(pred, 'member', 0, 0, tiled=True)]
  transfers between devices with their start and end apart: 11 -> 12, of which waited for: 6 -> 6; matrix products, arithmetic and copies ran while one was open for 1% -> 1% of each run, Pallas kernels for 2% -> 2%
where the time goes in v3:
time: 99.7 us; the launch traced here: 99.1 us
  starting transfers between devices  42.7 us (43%)
  blocking collectives  23.4 us (23%)
  waiting for transfers between devices  22.6 us (23%)
  Pallas kernels  5.11 us (5%)
  between operations  2.81 us (3%)
  other arithmetic  2.36 us (2%)
    all_to_all x1, blocking collectives, body(): lax.all_to_all(partial, AXES, 0, 0, axis_index_groups=mean_groups(), tile...  23.4 us
    ppermute x5, starting transfers between devices, swap(): return lax.ppermute(block, AXES, pairing(partner, step))  17.1 us
    ppermute x5, waiting for transfers between devices, swap(): return lax.ppermute(block, AXES, pairing(partner, step))  11.3 us
    ppermute x1, starting transfers between devices, body(): other = lax.ppermute(mine, 'lat', on_chip)  9.77 us
    ppermute x1, waiting for transfers between devices, body(): far = lax.ppermute(far, AXES, onward)  6.19 us
    all_to_all x1, waiting for transfers between devices, body(): fields = lax.all_to_all(pred, 'member', 0, 0, tiled=True)  5.1 us
    ppermute x1, starting transfers between devices, body(): first_o = lax.ppermute(first_b, 'lat', on_chip)  3.97 us
    all_to_all x1, starting transfers between devices, body(): fields = lax.all_to_all(pred, 'member', 0, 0, tiled=True)  3.51 us
  transfers between devices with their start and end apart: 12, of which 6 were waited for; matrix products, arithmetic and copies ran while one was open for 1% of the time, Pallas kernels for 2%

profile of v3, /device:TPU:1, one launch (start us, length us, event | category | flops | bytes accessed | tf_op | source)
XLA Modules:
  0.0 99.1 jit_solution(16841779658677683345)
XLA Ops:
  0.6 0.8 fusion.2
  1.5 5.9 %collective-permute-start.3 = (bf16[2,1,144,128]{3,2,1,0:T(8,128)(2,1)S(1)}, bf16[2,1,144,128]{3,2,1,0:T(8,128)(2,1)S(1)}, u32[]{:S(2)}, u32[]{:S(2)}) collective-permute-start(bf16[2,1,144,128]{3,2,1,0:T(8,128)(2,1)S(1)} %fusion.2), channel_id=1, source_target_pairs={{0,32},{1,99},{2,34},{3,97},{4,36},{5,103},{6,38},{7,101},{8,40},{... | collective-permute-start | bytes 221192 | tf_op jit(solution)/shard_map/ppermute | solution.py:37
  7.4 1.7 %collective-permute-done.3 = bf16[2,1,144,128]{3,2,1,0:T(8,128)(2,1)S(1)} collective-permute-done((bf16[2,1,144,128]{3,2,1,0:T(8,128)(2,1)S(1)}, bf16[2,1,144,128]{3,2,1,0:T(8,128)(2,1)S(1)}, u32[]{:S(2)}, u32[]{:S(2)}) %collective-permute-start.3) | collective-permute-done | bytes 73760 | tf_op jit(solution)/shard_map/ppermute | solution.py:37
  9.2 1.9 %collective-permute-start.4 = (bf16[2,2,144,128]{3,2,1,0:T(8,128)(2,1)S(1)}, bf16[2,2,144,128]{3,2,1,0:T(8,128)(2,1)S(1)}, u32[]{:S(2)}, u32[]{:S(2)}) collective-permute-start(bf16[2,2,144,128]{3,2,1,0:T(8,128)(2,1)S(1)} %pad_maximum_fusion.2), channel_id=1, source_target_pairs={{0,98},{1,33},{2,96},{3,35},{4,102},{5,37},{6,100},{7,39},{8,106},... | collective-permute-start | bytes 442376 | tf_op jit(solution)/shard_map/ppermute | solution.py:37
  11.1 4.4 %collective-permute-done.4 = bf16[2,2,144,128]{3,2,1,0:T(8,128)(2,1)S(1)} collective-permute-done((bf16[2,2,144,128]{3,2,1,0:T(8,128)(2,1)S(1)}, bf16[2,2,144,128]{3,2,1,0:T(8,128)(2,1)S(1)}, u32[]{:S(2)}, u32[]{:S(2)}) %collective-permute-start.4) | collective-permute-done | bytes 147488 | tf_op jit(solution)/shard_map/ppermute | solution.py:37
  15.5 4.0 %collective-permute-start.5 = (bf16[2,4,144,128]{3,2,1,0:T(8,128)(2,1)S(1)}, bf16[2,4,144,128]{3,2,1,0:T(8,128)(2,1)S(1)}, u32[]{:S(2)}, u32[]{:S(2)}) collective-permute-start(bf16[2,4,144,128]{3,2,1,0:T(8,128)(2,1)S(1)} %pad_maximum_fusion.1), channel_id=1, source_target_pairs={{0,128},{1,385},{2,130},{3,387},{4,132},{5,389},{6,134},{7,391},{8... | collective-permute-start | bytes 884744 | tf_op jit(solution)/shard_map/ppermute | solution.py:37
  19.5 4.7 %collective-permute-done.5 = bf16[2,4,144,128]{3,2,1,0:T(8,128)(2,1)S(1)} collective-permute-done((bf16[2,4,144,128]{3,2,1,0:T(8,128)(2,1)S(1)}, bf16[2,4,144,128]{3,2,1,0:T(8,128)(2,1)S(1)}, u32[]{:S(2)}, u32[]{:S(2)}) %collective-permute-start.5) | collective-permute-done | bytes 294944 | tf_op jit(solution)/shard_map/ppermute | solution.py:37
  24.3 9.8 %collective-permute-start.7 = (bf16[2,8,144,128]{3,2,1,0:T(8,128)(2,1)S(1)}, bf16[2,8,144,128]{3,2,1,0:T(8,128)(2,1)S(1)}, u32[]{:S(2)}, u32[]{:S(2)}) collective-permute-start(bf16[2,8,144,128]{3,2,1,0:T(8,128)(2,1)S(1)} %pad_maximum_fusion.mine_a), channel_id=1, source_target_pairs={{0,1},{1,0},{2,3},{3,2},{4,5},{5,4},{6,7},{7,6},{8,9},{9,8},{10,11... | collective-permute-start | bytes 1769480 | tf_op jit(solution)/shard_map/ppermute | solution.py:195
  34.1 1.9 %collective-permute-start.6 = (bf16[8,144,128]{2,1,0:T(8,128)(2,1)S(1)}, bf16[8,144,128]{2,1,0:T(8,128)(2,1)S(1)}, u32[]{:S(2)}, u32[]{:S(2)}) collective-permute-start(bf16[8,144,128]{2,1,0:T(8,128)(2,1)S(1)} %get-tuple-element.7), channel_id=1, source_target_pairs={{0,384},{1,129},{2,386},{3,131},{4,388},{5,133},{6,390},{7,135},{8... | collective-permute-start | bytes 884744 | tf_op jit(solution)/shard_map/ppermute | solution.py:37
  36.0 1.9 %collective-permute-start.1 = (bf16[2,256,256]{2,1,0:T(8,128)(2,1)S(1)}, bf16[2,256,256]{2,1,0:T(8,128)(2,1)S(1)}, u32[]{:S(2)}, u32[]{:S(2)}) collective-permute-start(bf16[2,256,256]{2,1,0:T(8,128)(2,1)S(1)} %bitcast.13), channel_id=1, source_target_pairs={{0,66},{1,65},{2,64},{3,67},{4,70},{5,69},{6,68},{7,71},{8,74},{9,... | collective-permute-start | bytes 786440 | tf_op jit(solution)/shard_map/ppermute | solution.py:193
  38.0 3.4 %collective-permute-start.9 = (bf16[8,144,128]{2,1,0:T(8,128)(2,1)S(1)}, bf16[8,144,128]{2,1,0:T(8,128)(2,1)S(1)}, u32[]{:S(2)}, u32[]{:S(2)}) collective-permute-start(bf16[8,144,128]{2,1,0:T(8,128)(2,1)S(1)} %get-tuple-element.6), channel_id=1, source_target_pairs={{0,384},{1,129},{2,386},{3,131},{4,388},{5,133},{6,390},{7,135},{8... | collective-permute-start | bytes 884744 | tf_op jit(solution)/shard_map/ppermute | solution.py:37
  41.9 4.0 %collective-permute-start.8 = (bf16[8,144,128]{2,1,0:T(8,128)(2,1)S(1)}, bf16[8,144,128]{2,1,0:T(8,128)(2,1)S(1)}, u32[]{:S(2)}, u32[]{:S(2)}) collective-permute-start(bf16[8,144,128]{2,1,0:T(8,128)(2,1)S(1)} %collective-permute-done.6.mine_b), channel_id=1, source_target_pairs={{0,1},{1,0},{2,3},{3,2},{4,5},{5,4},{6,7},{7,6},{8,9},{9,8},{10,11... | collective-permute-start | bytes 884744 | tf_op jit(solution)/shard_map/ppermute | solution.py:196
  45.8 1.9 %collective-permute-start = (bf16[2,256,256]{2,1,0:T(8,128)(2,1)S(1)}, bf16[2,256,256]{2,1,0:T(8,128)(2,1)S(1)}, u32[]{:S(2)}, u32[]{:S(2)}) collective-permute-start(bf16[2,256,256]{2,1,0:T(8,128)(2,1)S(1)} %bitcast.14), channel_id=1, source_target_pairs={{0,1},{1,0},{2,3},{3,2},{4,5},{5,4},{6,7},{7,6},{8,9},{9,8},{10,11... | collective-permute-start | bytes 786440 | tf_op jit(solution)/shard_map/ppermute | solution.py:191
  47.8 2.6 %collective-permute-start.2 = (bf16[2,256,256]{2,1,0:T(8,128)(2,1)S(1)}, bf16[2,256,256]{2,1,0:T(8,128)(2,1)S(1)}, u32[]{:S(2)}, u32[]{:S(2)}) collective-permute-start(bf16[2,256,256]{2,1,0:T(8,128)(2,1)S(1)} %collective-permute-done.1), channel_id=1, source_target_pairs={{65,2},{64,1},{67,4},{70,3},{69,6},{68,5},{71,8},{74,7},{73,10},{7... | collective-permute-start | bytes 786440 | tf_op jit(solution)/shard_map/ppermute | solution.py:194
  50.4 1.9 %collective-permute-start.10 = (bf16[8,144,128]{2,1,0:T(8,128)(2,1)S(1)}, bf16[8,144,128]{2,1,0:T(8,128)(2,1)S(1)}, u32[]{:S(2)}, u32[]{:S(2)}) collective-permute-start(bf16[8,144,128]{2,1,0:T(8,128)(2,1)S(1)} %collective-permute-done.9.mine_b), channel_id=1, source_target_pairs={{0,1},{1,0},{2,3},{3,2},{4,5},{5,4},{6,7},{7,6},{8,9},{9,8},{10,11... | collective-permute-start | bytes 884744 | tf_op jit(solution)/shard_map/ppermute | solution.py:197
  53.0 6.2 %collective-permute-done.2.far = bf16[2,256,256]{2,1,0:T(8,128)(2,1)S(1)} collective-permute-done((bf16[2,256,256]{2,1,0:T(8,128)(2,1)S(1)}, bf16[2,256,256]{2,1,0:T(8,128)(2,1)S(1)}, u32[]{:S(2)}, u32[]{:S(2)}) %collective-permute-start.2) | collective-permute-done | bytes 262176 | tf_op jit(solution)/shard_map/ppermute | solution.py:194
  59.2 2.0 %first.1.inner = bf16[4,256,256]{2,1,0:T(8,128)(2,1)S(1)} custom-call(s32[1]{0:T(128)S(6)} %copy.10.ident, f32[16,256]{1,0:T(8,128)S(1)} %copy-done.1, bf16[2,256,256]{2,1,0:T(8,128)(2,1)S(1)} %bitcast.15, bf16[2,256,256]{2,1,0:T(8,128)(2,1)S(1)} %collective-permute-done.near, bf16[2,256,256]{2,1,0:T(8,128)(2,1)S(1)} %collective-permute-done.2.far, ...), custom_call_target="tpu_custom_call" | custom-call | flops 1207959552 | bytes 4194304 | tf_op jit(solution)/shard_map/first/pallas_call | solution.py:199
  61.2 1.7 %second.1 = bf16[16,8,512]{2,1,0:T(8,128)(2,1)} custom-call(s32[1]{0:T(128)S(6)} %copy.10.ident, f32[16,256]{1,0:T(8,128)S(1)} %copy-done.1, bf16[2,256,256]{2,1,0:T(8,128)(2,1)S(1)} %bitcast.16, bf16[4,256,256]{2,1,0:T(8,128)(2,1)S(1)} %first.1.inner, bf16[8,256]{1,0:T(8,128)(2,1)S(1)} %bitcast.17, bf16[2,8,144,128]{3,2,1,0:T(8,128)(2,1)S(1)} %pad_maximum_fusion.mine_a, ...), custom_call_target="tpu_custom_call" | custom-call | flops 603979776 | bytes 3145728 | tf_op jit(solution)/shard_map/second/pallas_call | solution.py:214
  63.0 3.5 %all-to-all-start = ((bf16[16,8,512]{2,1,0:T(8,128)(2,1)}), bf16[16,8,512]{2,1,0:T(8,128)(2,1)S(1)}, u32[]{:S(2)}, u32[]{:S(2)}) async-start(bf16[16,8,512]{2,1,0:T(8,128)(2,1)} %second.1), calls=%async_computation | async-start | bytes 262144 | tf_op jit(solution)/shard_map/all_to_all | solution.py:229
  67.1 0.6 fusion.3
  68.6 5.1 %all-to-all-done.fields = bf16[16,8,512]{2,1,0:T(8,128)(2,1)S(1)} async-done(((bf16[16,8,512]{2,1,0:T(8,128)(2,1)}), bf16[16,8,512]{2,1,0:T(8,128)(2,1)S(1)}, u32[]{:S(2)}, u32[]{:S(2)}) %all-to-all-start) | async-done | bytes 131104 | tf_op jit(solution)/shard_map/all_to_all | solution.py:229
  73.7 1.4 %score.1 = (f32[8,2,256]{2,1,0:T(2,128)}, f32[32,1,128]{2,1,0:T(1,128)S(1)}) custom-call(f32[2]{0:T(128)S(1)} %dynamic-slice_divide_fusion.weight, bf16[16,8,512]{2,1,0:T(8,128)(2,1)S(1)} %all-to-all-done.fields, f32[8,2,256]{2,1,0:T(2,128)S(1)} %copy-done.2), custom_call_target="tpu_custom_call" | custom-call | tf_op jit(solution)/shard_map/score/pallas_call | solution.py:238
  75.1 23.4 %all_to_all.10 = f32[32,1,128]{2,1,0:T(1,128)S(1)} all-to-all(f32[32,1,128]{2,1,0:T(1,128)S(1)} %get-tuple-element.5), channel_id=1, replica_groups={{0,1,66,67,4,5,70,71,8,9,74,75,12,13,78,79,16,17,82,83,20,21,86,87,24,2..., dimensions={0} | all-to-all | bytes 32768 | tf_op jit(solution)/shard_map/all_to_all | solution.py:249
  98.5 0.6 slice_reduce_fusion
  (21 shorter events, 0.8 us)
Async XLA Ops:
  1.5 7.7 %collective-permute-start.3 = (bf16[2,1,144,128]{3,2,1,0:T(8,128)(2,1)S(1)}, bf16[2,1,144,128]{3,2,1,0:T(8,128)(2,1)S(1)}, u32[]{:S(2)}, u32[]{:S(2)}) collective-permute-start(bf16[2,1,144,128]{3,2,1,0:T(8,128)(2,1)S(1)} %fusion.2), channel_id=1, source_target_pairs={{0,32},{1,99},{2,34},{3,97},{4,36},{5,103},{6,38},{7,101},{8,40},{... | collective-permute-start | bytes 221192 | tf_op jit(solution)/shard_map/ppermute | solution.py:37
  9.2 6.3 %collective-permute-start.4 = (bf16[2,2,144,128]{3,2,1,0:T(8,128)(2,1)S(1)}, bf16[2,2,144,128]{3,2,1,0:T(8,128)(2,1)S(1)}, u32[]{:S(2)}, u32[]{:S(2)}) collective-permute-start(bf16[2,2,144,128]{3,2,1,0:T(8,128)(2,1)S(1)} %pad_maximum_fusion.2), channel_id=1, source_target_pairs={{0,98},{1,33},{2,96},{3,35},{4,102},{5,37},{6,100},{7,39},{8,106},... | collective-permute-start | bytes 442376 | tf_op jit(solution)/shard_map/ppermute | solution.py:37
  15.5 8.7 %collective-permute-start.5 = (bf16[2,4,144,128]{3,2,1,0:T(8,128)(2,1)S(1)}, bf16[2,4,144,128]{3,2,1,0:T(8,128)(2,1)S(1)}, u32[]{:S(2)}, u32[]{:S(2)}) collective-permute-start(bf16[2,4,144,128]{3,2,1,0:T(8,128)(2,1)S(1)} %pad_maximum_fusion.1), channel_id=1, source_target_pairs={{0,128},{1,385},{2,130},{3,387},{4,132},{5,389},{6,134},{7,391},{8... | collective-permute-start | bytes 884744 | tf_op jit(solution)/shard_map/ppermute | solution.py:37
  24.2 11.8 %copy-start = (bf16[1,2,256,256]{3,2,1,0:T(8,128)(2,1)S(1)}, bf16[1,2,256,256]{3,2,1,0:T(8,128)(2,1)}, u32[]{:S(2)}) copy-start(bf16[1,2,256,256]{3,2,1,0:T(8,128)(2,1)} %param.8) | copy-start | bytes 786436
  24.3 34.9 %copy-start.1 = (f32[16,256]{1,0:T(8,128)S(1)}, f32[16,256]{1,0:T(8,128)}, u32[]{:S(2)}) copy-start(f32[16,256]{1,0:T(8,128)} %gains.3) | copy-start | bytes 49156
  24.3 34.9 %collective-permute-start.7 = (bf16[2,8,144,128]{3,2,1,0:T(8,128)(2,1)S(1)}, bf16[2,8,144,128]{3,2,1,0:T(8,128)(2,1)S(1)}, u32[]{:S(2)}, u32[]{:S(2)}) collective-permute-start(bf16[2,8,144,128]{3,2,1,0:T(8,128)(2,1)S(1)} %pad_maximum_fusion.mine_a), channel_id=1, source_target_pairs={{0,1},{1,0},{2,3},{3,2},{4,5},{5,4},{6,7},{7,6},{8,9},{9,8},{10,11... | collective-permute-start | bytes 1769480 | tf_op jit(solution)/shard_map/ppermute | solution.py:195
  34.1 7.8 %collective-permute-start.6 = (bf16[8,144,128]{2,1,0:T(8,128)(2,1)S(1)}, bf16[8,144,128]{2,1,0:T(8,128)(2,1)S(1)}, u32[]{:S(2)}, u32[]{:S(2)}) collective-permute-start(bf16[8,144,128]{2,1,0:T(8,128)(2,1)S(1)} %get-tuple-element.7), channel_id=1, source_target_pairs={{0,384},{1,129},{2,386},{3,131},{4,388},{5,133},{6,390},{7,135},{8... | collective-permute-start | bytes 884744 | tf_op jit(solution)/shard_map/ppermute | solution.py:37
  36.0 11.7 %collective-permute-start.1 = (bf16[2,256,256]{2,1,0:T(8,128)(2,1)S(1)}, bf16[2,256,256]{2,1,0:T(8,128)(2,1)S(1)}, u32[]{:S(2)}, u32[]{:S(2)}) collective-permute-start(bf16[2,256,256]{2,1,0:T(8,128)(2,1)S(1)} %bitcast.13), channel_id=1, source_target_pairs={{0,66},{1,65},{2,64},{3,67},{4,70},{5,69},{6,68},{7,71},{8,74},{9,... | collective-permute-start | bytes 786440 | tf_op jit(solution)/shard_map/ppermute | solution.py:193
  38.0 12.4 %collective-permute-start.9 = (bf16[8,144,128]{2,1,0:T(8,128)(2,1)S(1)}, bf16[8,144,128]{2,1,0:T(8,128)(2,1)S(1)}, u32[]{:S(2)}, u32[]{:S(2)}) collective-permute-start(bf16[8,144,128]{2,1,0:T(8,128)(2,1)S(1)} %get-tuple-element.6), channel_id=1, source_target_pairs={{0,384},{1,129},{2,386},{3,131},{4,388},{5,133},{6,390},{7,135},{8... | collective-permute-start | bytes 884744 | tf_op jit(solution)/shard_map/ppermute | solution.py:37
  41.9 17.3 %collective-permute-start.8 = (bf16[8,144,128]{2,1,0:T(8,128)(2,1)S(1)}, bf16[8,144,128]{2,1,0:T(8,128)(2,1)S(1)}, u32[]{:S(2)}, u32[]{:S(2)}) collective-permute-start(bf16[8,144,128]{2,1,0:T(8,128)(2,1)S(1)} %collective-permute-done.6.mine_b), channel_id=1, source_target_pairs={{0,1},{1,0},{2,3},{3,2},{4,5},{5,4},{6,7},{7,6},{8,9},{9,8},{10,11... | collective-permute-start | bytes 884744 | tf_op jit(solution)/shard_map/ppermute | solution.py:196
  45.8 7.1 %collective-permute-start = (bf16[2,256,256]{2,1,0:T(8,128)(2,1)S(1)}, bf16[2,256,256]{2,1,0:T(8,128)(2,1)S(1)}, u32[]{:S(2)}, u32[]{:S(2)}) collective-permute-start(bf16[2,256,256]{2,1,0:T(8,128)(2,1)S(1)} %bitcast.14), channel_id=1, source_target_pairs={{0,1},{1,0},{2,3},{3,2},{4,5},{5,4},{6,7},{7,6},{8,9},{9,8},{10,11... | collective-permute-start | bytes 786440 | tf_op jit(solution)/shard_map/ppermute | solution.py:191
  47.8 11.4 %collective-permute-start.2 = (bf16[2,256,256]{2,1,0:T(8,128)(2,1)S(1)}, bf16[2,256,256]{2,1,0:T(8,128)(2,1)S(1)}, u32[]{:S(2)}, u32[]{:S(2)}) collective-permute-start(bf16[2,256,256]{2,1,0:T(8,128)(2,1)S(1)} %collective-permute-done.1), channel_id=1, source_target_pairs={{65,2},{64,1},{67,4},{70,3},{69,6},{68,5},{71,8},{74,7},{73,10},{7... | collective-permute-start | bytes 786440 | tf_op jit(solution)/shard_map/ppermute | solution.py:194
  50.4 10.8 %collective-permute-start.10 = (bf16[8,144,128]{2,1,0:T(8,128)(2,1)S(1)}, bf16[8,144,128]{2,1,0:T(8,128)(2,1)S(1)}, u32[]{:S(2)}, u32[]{:S(2)}) collective-permute-start(bf16[8,144,128]{2,1,0:T(8,128)(2,1)S(1)} %collective-permute-done.9.mine_b), channel_id=1, source_target_pairs={{0,1},{1,0},{2,3},{3,2},{4,5},{5,4},{6,7},{7,6},{8,9},{9,8},{10,11... | collective-permute-start | bytes 884744 | tf_op jit(solution)/shard_map/ppermute | solution.py:197
  59.2 2.0 %copy-start.3 = (bf16[256,8]{0,1:T(8,128)(2,1)S(1)}, bf16[256,8]{0,1:T(8,128)(2,1)}, u32[]{:S(2)}) copy-start(bf16[256,8]{0,1:T(8,128)(2,1)} %param.13) | copy-start | bytes 12292
  63.0 10.7 %all-to-all-start = ((bf16[16,8,512]{2,1,0:T(8,128)(2,1)}), bf16[16,8,512]{2,1,0:T(8,128)(2,1)S(1)}, u32[]{:S(2)}, u32[]{:S(2)}) async-start(bf16[16,8,512]{2,1,0:T(8,128)(2,1)} %second.1), calls=%async_computation | async-start | bytes 262144 | tf_op jit(solution)/shard_map/all_to_all | solution.py:229
  66.5 7.2 %copy-start.2 = (f32[8,2,256]{2,1,0:T(2,128)S(1)}, f32[8,2,256]{2,1,0:T(2,128)}, u32[]{:S(2)}) copy-start(f32[8,2,256]{2,1,0:T(2,128)} %target.1) | copy-start | bytes 49156
